TPU v7x, 32 devices: a whole 2x2x4 slice. The times are simulated.
32 devices in a mesh: land: 2 (over x), dp: 16 (over z, y, core).
Axes of the slice: x: 2, y: 2, z: 4, core: 2. Of those that a mesh axis runs over, the one named last changes fastest.
Arguments:
- embeddings: bfloat16 [8192, 1280], P(('dp', 'land')), may hold values from -6 to 6
- landmarks: bfloat16 [2048, 1280], P(('land', 'dp')), may hold values from -6 to 6
- factor: bfloat16 [2048, 1024], P(('land', 'dp')), may hold values from -6 to 6
- centroids: bfloat16 [4096, 1024], P('land'), may hold values from -6 to 6
- assignment: int32 [8192], P('dp'), may hold values from 0 to 4095, as said below
Outputs:
- distances: float32 [8192, 4096], P('dp', 'land')
- new_centroids: float32 [4096, 1024], P(('land', 'dp'))
Inputs may be any that keep to these rules, and one draw needn't show every extreme that they name: `assignment`: among the 512 rows of one index of dp, at most 32 are assigned to centroids of any one aligned block of 128 centroid numbers.
All inputs are finite; a program needn't handle non-finite values.
Results may differ from a plain program's by a relative error of at most 0.01.
Values may be sent and summed in bfloat16 or wider, within the bound.
No kernel may reach another device: no remote copies, remote signals or barrier semaphores. Data moves between devices by JAX's collectives and lax.ppermute only.
A program may use at most 64 MiB of HBM per device.

v0:
```python
import functools

import jax
import jax.numpy as jnp
from jax import lax
from jax.experimental import pallas as pl
from jax.experimental.pallas import tpu as pltpu
from jax.sharding import PartitionSpec as P


EPSILON = 1e-06
SHARPNESS = 6.0
FACTOR_PARTS = 2
VMEM = pl.BlockSpec(memory_space=pltpu.VMEM)
SMEM = pl.BlockSpec(memory_space=pltpu.SMEM)


def split_dp(count):
    cores = 2 if count % 2 == 0 else 1
    outer = 4 if (count // cores) % 4 == 0 else 1
    return outer, count // cores // outer, cores


def partner(index, size, step):
    return index ^ step if size & (size - 1) == 0 else (index + step) % size


def axis_perm(sizes, axis, step):
    outer, middle, cores = sizes
    pairs = []
    for z in range(outer):
        for y in range(middle):
            for c in range(cores):
                target = [z, y, c]
                target[axis] = partner(target[axis], sizes[axis], step)
                pairs.append(((z * middle + y) * cores + c, (target[0] * middle + target[1]) * cores + target[2]))
    return pairs


def call(body, outs, args, land, scratch=(), flops=0, limit=24):
    moved = sum(a.size * a.dtype.itemsize for a in list(args) + list(outs))
    return pl.pallas_call(
        body,
        out_shape=list(outs),
        in_specs=[SMEM] + [VMEM] * len(args),
        out_specs=[VMEM] * len(outs),
        scratch_shapes=[pltpu.VMEM(*s) for s in scratch],
        cost_estimate=pl.CostEstimate(flops=flops, bytes_accessed=moved, transcendentals=0),
        compiler_params=pltpu.CompilerParams(vmem_limit_bytes=limit * 2**20),
    )(land, *args)


def column_to_row(column):
    wide = jnp.broadcast_to(column, (column.shape[0], 128))
    return jnp.transpose(wide)[0:1]


def kernel_body(land_count, cores, pieces, land_ref, *refs):
    count = land_count * cores
    row_refs, mark_refs = refs[:count], refs[count : count + pieces]
    out_ref, marks = refs[count + pieces :]
    depth, width = mark_refs[0].shape
    rows = row_refs[0].shape[0]
    for i, piece in enumerate(mark_refs):
        marks[i * depth : (i + 1) * depth] = piece[...]
    square = jnp.square(marks[...].astype(jnp.float32))
    mark_scale = column_to_row(lax.rsqrt(jnp.sum(square, axis=1, keepdims=True) / width + EPSILON))
    for g in range(cores):
        for s in range(land_count):
            source = lax.rem(land_ref[0] + s, land_count)
            values = row_refs[g * land_count + s][...]
            square = jnp.square(values.astype(jnp.float32))
            scale = lax.rsqrt(jnp.sum(square, axis=1, keepdims=True) / width + EPSILON) / width
            dots = lax.dot_general(values, marks[...], (((1,), (1,)), ((), ())), preferred_element_type=jnp.float32)
            similarity = dots * scale * mark_scale
            offset = pl.multiple_of(g * land_count * rows + source * rows, rows)
            out_ref[pl.ds(offset, rows), :] = jnp.exp(SHARPNESS * (similarity - 1.0)).astype(out_ref.dtype)


def partial_body(land_count, cores, pieces, part, land_ref, kern_ref, *refs):
    piece_refs, (own_ref, *others, block) = refs[:pieces], refs[pieces:]
    depth, full = piece_refs[0].shape
    keep_width = full // land_count
    width = block.shape[1]
    rows = own_ref.shape[0]
    for s in range(land_count):
        source = lax.rem(land_ref[0] + s, land_count)
        columns = pl.ds(pl.multiple_of(source * keep_width + part * width, 128), width)
        for i, piece in enumerate(piece_refs):
            block[i * depth : (i + 1) * depth] = piece[:, columns]
        for g in reversed(range(cores)):
            out = own_ref if g == 0 else others[g - 1]
            value = jnp.dot(kern_ref[g * rows : (g + 1) * rows], block[...], preferred_element_type=jnp.float32)
            out[:, s * width : (s + 1) * width] = value.astype(out.dtype)


def add_body(count, land_ref, *refs):
    ins, outs = refs[:count], refs[count:]
    width = outs[0].shape[1]
    for s, out in enumerate(outs):
        total = ins[0][:, s * width : (s + 1) * width]
        for part in ins[1:]:
            total = total + part[:, s * width : (s + 1) * width].astype(jnp.float32)
        out[...] = total.astype(out.dtype)


def pick_body(count, land_ref, *refs):
    *ins, pick_ref, feat_ref, out_ref = refs
    total = ins[0][...].astype(jnp.float32)
    for part in ins[1:count]:
        total = total + part[...].astype(jnp.float32)
    features = total.astype(feat_ref.dtype)
    feat_ref[...] = features
    start = 0
    for done in ins[count:]:
        start = done.shape[1]
        out_ref[:, :start] = done[...]
    value = jnp.dot(pick_ref[...], features, preferred_element_type=jnp.float32)
    out_ref[:, start:] = value.astype(out_ref.dtype)


def distance_body(land_count, parts, land_ref, *refs):
    count = land_count * parts
    feats, cent_ref, out_ref, feat_sq = refs[:count], refs[count], refs[count + 1], refs[count + 2]

    @pl.when(pl.program_id(0) == 0)
    def _():
        total = jnp.zeros(feat_sq.shape, jnp.float32)
        for feat in feats:
            total = total + jnp.sum(jnp.square(feat[...].astype(jnp.float32)), axis=1, keepdims=True)
        feat_sq[...] = total

    cent = cent_ref[...]
    cent_sq = column_to_row(jnp.sum(jnp.square(cent.astype(jnp.float32)), axis=1, keepdims=True))
    width = feats[0].shape[1]
    cross = None
    for s in range(land_count):
        source = lax.rem(land_ref[0] + s, land_count)
        for h in range(parts):
            columns = pl.ds(pl.multiple_of((source * parts + h) * width, 128), width)
            term = lax.dot_general(
                feats[s * parts + h][...],
                cent_ref[:, columns],
                (((1,), (1,)), ((), ())),
                preferred_element_type=jnp.float32,
            )
            cross = term if cross is None else cross + term
    out_ref[...] = (feat_sq[...] + cent_sq - 2.0 * cross) / cent_ref.shape[1]


def mean_body(land_count, land_ref, ids_ref, arrived_ref, out_ref):
    own_width, width = out_ref.shape[0], arrived_ref.shape[1]
    slots = ids_ref.shape[1] // land_count
    for j in range(land_count):
        match = ids_ref[:, j * slots : (j + 1) * slots] == lax.broadcasted_iota(jnp.int32, (own_width, slots), 0)
        match = match.astype(jnp.float32)
        counts = jnp.sum(match, axis=1, keepdims=True)
        part = arrived_ref[j * slots : (j + 1) * slots]
        sums = jnp.dot(match.astype(jnp.bfloat16), part, preferred_element_type=jnp.float32)
        out_ref[:, j * width : (j + 1) * width] = sums / jnp.maximum(counts, 1.0)


def factor_parts(feat_width, land_count):
    return FACTOR_PARTS if feat_width % (128 * land_count * FACTOR_PARTS) == 0 else 1


def local(embeddings, landmarks, factor, centroids, assignment):
    land_count = lax.axis_size("land")
    dp_count = lax.axis_size("dp")
    land_id = lax.axis_index("land")
    land = land_id.astype(jnp.int32).reshape(1)
    sizes = split_dp(dp_count)
    cores = sizes[2]
    own_rows, embed_width = embeddings.shape
    feat_width = factor.shape[1]
    group_rows = own_rows * land_count
    bf16, f32 = jnp.bfloat16, jnp.float32

    def shape(rows, columns, dtype):
        return jax.ShapeDtypeStruct((rows, columns), dtype)

    def move(x, axis, step):
        return lax.ppermute(x, "dp", axis_perm(sizes, axis, step))

    def land_send(x, step):
        return lax.ppermute(x, "land", [(s, (s + step) % land_count) for s in range(land_count)])

    def outer_shifts(x):
        return [x] + [move(x, 0, k) for k in range(1, sizes[0])]

    def middle_shifts(pieces):
        return pieces + [move(p, 1, k) for p in pieces for k in range(1, sizes[1])]

    row_pieces = [embeddings] + [land_send(embeddings, land_count - k) for k in range(1, land_count)]
    row_pieces = row_pieces + [move(p, 2, k) for k in range(1, cores) for p in row_pieces]
    marks = middle_shifts(outer_shifts(landmarks))
    parts = factor_parts(feat_width, land_count)
    keep_width = feat_width // land_count
    width = keep_width // parts
    factors = middle_shifts(outer_shifts(factor))

    rows_all = group_rows * cores
    depth_all = landmarks.shape[0] * len(marks)
    (kern,) = call(
        functools.partial(kernel_body, land_count, cores, len(marks)),
        [shape(rows_all, depth_all, bf16)],
        row_pieces + marks,
        land,
        scratch=[((depth_all, embed_width), bf16)],
        flops=2 * rows_all * depth_all * embed_width,
    )
    keeps, sends = [], []
    for h in range(parts):
        own, *others = call(
            functools.partial(partial_body, land_count, cores, len(marks), h),
            [shape(group_rows, land_count * width, f32)]
            + [shape(group_rows, land_count * width, bf16)] * (cores - 1),
            [kern] + factors,
            land,
            scratch=[((depth_all, width), bf16)],
            flops=2 * rows_all * depth_all * land_count * width,
        )
        others = [move(o, 2, cores - g) for g, o in enumerate(others, 1)]
        keep, *send = call(
            functools.partial(add_body, cores), [shape(group_rows, width, bf16)] * land_count, [own] + others, land
        )
        keeps.append(keep)
        sends.append([land_send(x, s) for s, x in enumerate(send, 1)])

    own_width = centroids.shape[0] // dp_count
    slot_count = 2 * max(1, group_rows // (land_count * dp_count))
    slot_total = land_count * dp_count * slot_count
    everyone = ("land", "dp")
    slice_id = assignment // own_width
    local_id = assignment % own_width
    row_pos = lax.iota(jnp.int32, group_rows)
    earlier = (slice_id[None, :] == slice_id[:, None]) & (row_pos[None, :] < row_pos[:, None])
    slot_rank = jnp.sum(earlier.astype(jnp.int32), axis=1)
    slot_of = slice_id * slot_count + slot_rank
    slot_match = lax.iota(jnp.int32, slot_total)[:, None] == slot_of[None, :]
    slot_ids = jnp.max(jnp.where(slot_match, local_id[None, :], -1), axis=1)
    slot_pick = slot_match.astype(bf16)
    arrived_ids = lax.all_to_all(
        slot_ids.reshape(land_count * dp_count, slot_count), everyone, split_axis=0, concat_axis=0, tiled=True
    )
    arrived_ids = arrived_ids.reshape(1, slot_total)

    mine, outgoing = [], None
    for h in range(parts):
        before = [outgoing] if h else []
        feat, outgoing = call(
            functools.partial(pick_body, land_count),
            [shape(group_rows, width, bf16), shape(slot_total, (h + 1) * width, bf16)],
            [keeps[h]] + sends[h] + before + [slot_pick],
            land,
            flops=2 * group_rows * slot_total * width,
        )
        mine.append(feat)
    arrived = lax.all_to_all(
        outgoing.reshape(land_count * dp_count, slot_count, keep_width),
        everyone,
        split_axis=0,
        concat_axis=0,
        tiled=True,
    )
    arrived = arrived.reshape(slot_total, keep_width)
    feats = mine + [land_send(mine[h], land_count - s) for s in range(1, land_count) for h in range(parts)]

    cent_block = centroids.shape[0]
    block = min(256, cent_block)
    distances = pl.pallas_call(
        functools.partial(distance_body, land_count, parts),
        grid=(cent_block // block,),
        out_shape=shape(group_rows, cent_block, f32),
        in_specs=[SMEM]
        + [pl.BlockSpec((group_rows, width), lambda i: (0, 0))] * len(feats)
        + [pl.BlockSpec((block, feat_width), lambda i: (i, 0))],
        out_specs=pl.BlockSpec((group_rows, block), lambda i: (0, i)),
        scratch_shapes=[pltpu.VMEM((group_rows, 1), f32)],
        cost_estimate=pl.CostEstimate(
            flops=2 * group_rows * cent_block * feat_width,
            bytes_accessed=2 * cent_block * feat_width + 4 * group_rows * cent_block,
            transcendentals=0,
        ),
        compiler_params=pltpu.CompilerParams(vmem_limit_bytes=24 * 2**20),
        name="distances",
    )(land, *feats, centroids)
    (new_centroids,) = call(
        functools.partial(mean_body, land_count),
        [shape(own_width, feat_width, f32)],
        [arrived_ids, arrived],
        land,
        flops=2 * own_width * slot_total * keep_width,
    )
    return (distances, new_centroids)


def solution(mesh):
    return jax.shard_map(
        local,
        mesh=mesh,
        in_specs=(
            P(("dp", "land"), None),
            P(("land", "dp"), None),
            P(("land", "dp"), None),
            P("land", None),
            P("dp"),
        ),
        out_specs=(P("dp", "land"), P(("land", "dp"), None)),
        check_vma=False,
    )
```

profile of v0, /device:TPU:9, one launch (start us, length us, event | category | flops | bytes accessed | tf_op | source)
XLA Modules:
  0.0 132.7 jit_solution(14583598560257660128)
XLA Ops:
  0.6 1.3 collective-permute-start
  1.9 1.0 collective-permute-start.1
  2.9 13.7 %collective-permute-done.refs_1_ = bf16[256,1280]{1,0:T(8,128)(2,1)S(1)} collective-permute-done((bf16[256,1280]{1,0:T(8,128)(2,1)}, bf16[256,1280]{1,0:T(8,128)(2,1)S(1)}, u32[]{:S(2)}, u32[]{:S(2)}) %collective-permute-start) | collective-permute-done | bytes 655392 | tf_op jit(solution)/shard_map/ppermute | solution.py:186
  16.5 1.5 %collective-permute-start.2 = (bf16[256,1280]{1,0:T(8,128)(2,1)S(1)}, bf16[256,1280]{1,0:T(8,128)(2,1)S(1)}, u32[]{:S(2)}, u32[]{:S(2)}) collective-permute-start(bf16[256,1280]{1,0:T(8,128)(2,1)S(1)} %collective-permute-done.refs_1_), channel_id=1, source_target_pairs={{0,1},{1,0},{2,3},{3,2},{4,5},{5,4},{6,7},{7,6},{8,9},{9,8},{10,11... | collective-permute-start | bytes 1966088 | tf_op jit(solution)/shard_map/ppermute | solution.py:183
  18.1 1.3 collective-permute-start.12
  19.4 0.2 collective-permute-start.5
  19.5 4.1 %collective-permute-start.11 = (bf16[64,1024]{1,0:T(8,128)(2,1)}, bf16[64,1024]{1,0:T(8,128)(2,1)S(1)}, u32[]{:S(2)}, u32[]{:S(2)}) collective-permute-start(bf16[64,1024]{1,0:T(8,128)(2,1)} %refs_0_.5), channel_id=1, source_target_pairs={{0,8},{1,9},{2,10},{3,11},{4,12},{5,13},{6,14},{7,15},{8,0},{9,1},... | collective-permute-start | bytes 393224 | tf_op jit(solution)/shard_map/ppermute | solution.py:183
  23.6 8.8 %collective-permute-done.12.refs_3_ = bf16[64,1024]{1,0:T(8,128)(2,1)S(1)} collective-permute-done((bf16[64,1024]{1,0:T(8,128)(2,1)}, bf16[64,1024]{1,0:T(8,128)(2,1)S(1)}, u32[]{:S(2)}, u32[]{:S(2)}) %collective-permute-start.12) | collective-permute-done | bytes 131104 | tf_op jit(solution)/shard_map/ppermute | solution.py:183
  32.4 0.0 collective-permute-start.10
  32.4 5.6 %collective-permute-done.11.refs_2_ = bf16[64,1024]{1,0:T(8,128)(2,1)S(1)} collective-permute-done((bf16[64,1024]{1,0:T(8,128)(2,1)}, bf16[64,1024]{1,0:T(8,128)(2,1)S(1)}, u32[]{:S(2)}, u32[]{:S(2)}) %collective-permute-start.11) | collective-permute-done | bytes 131104 | tf_op jit(solution)/shard_map/ppermute | solution.py:183
  38.0 3.0 %collective-permute-start.4 = (bf16[64,1280]{1,0:T(8,128)(2,1)}, bf16[64,1280]{1,0:T(8,128)(2,1)S(1)}, u32[]{:S(2)}, u32[]{:S(2)}) collective-permute-start(bf16[64,1280]{1,0:T(8,128)(2,1)} %refs_4_.2), channel_id=1, source_target_pairs={{0,8},{1,9},{2,10},{3,11},{4,12},{5,13},{6,14},{7,15},{8,0},{9,1},... | collective-permute-start | bytes 491528 | tf_op jit(solution)/shard_map/ppermute | solution.py:183
  41.0 1.3 collective-permute-start.6
  42.3 5.2 %collective-permute-done.4.refs_6_ = bf16[64,1280]{1,0:T(8,128)(2,1)S(1)} collective-permute-done((bf16[64,1280]{1,0:T(8,128)(2,1)}, bf16[64,1280]{1,0:T(8,128)(2,1)S(1)}, u32[]{:S(2)}, u32[]{:S(2)}) %collective-permute-start.4) | collective-permute-done | bytes 163872 | tf_op jit(solution)/shard_map/ppermute | solution.py:183
  47.5 1.2 collective-permute-start.9
  48.7 0.0 collective-permute-done.3.refs_5_
  48.7 0.2 collective-permute-start.8
  49.0 0.0 collective-permute-done.6.refs_8_
  49.0 1.2 collective-permute-start.7
  50.2 2.6 %collective-permute-done.9.refs_11_ = bf16[64,1280]{1,0:T(8,128)(2,1)S(1)} collective-permute-done((bf16[64,1280]{1,0:T(8,128)(2,1)S(1)}, bf16[64,1280]{1,0:T(8,128)(2,1)S(1)}, u32[]{:S(2)}, u32[]{:S(2)}) %collective-permute-start.9) | collective-permute-done | bytes 163872 | tf_op jit(solution)/shard_map/ppermute | solution.py:183
  52.8 0.7 copy-done.4
  53.4 1.2 collective-permute-start.13
  54.7 1.6 %collective-permute-done.8.refs_10_ = bf16[64,1280]{1,0:T(8,128)(2,1)S(1)} collective-permute-done((bf16[64,1280]{1,0:T(8,128)(2,1)S(1)}, bf16[64,1280]{1,0:T(8,128)(2,1)S(1)}, u32[]{:S(2)}, u32[]{:S(2)}) %collective-permute-start.8) | collective-permute-done | bytes 163872 | tf_op jit(solution)/shard_map/ppermute | solution.py:183
  56.3 0.7 copy-done.6
  57.0 1.2 collective-permute-start.16
  58.2 1.6 %collective-permute-done.7.refs_9_ = bf16[64,1280]{1,0:T(8,128)(2,1)S(1)} collective-permute-done((bf16[64,1280]{1,0:T(8,128)(2,1)S(1)}, bf16[64,1280]{1,0:T(8,128)(2,1)S(1)}, u32[]{:S(2)}, u32[]{:S(2)}) %collective-permute-start.7) | collective-permute-done | bytes 163872 | tf_op jit(solution)/shard_map/ppermute | solution.py:183
  59.8 0.7 copy-done.8
  60.5 1.2 collective-permute-start.15
  61.7 0.2 collective-permute-start.14
  61.9 1.1 copy-done.1
  63.0 0.9 copy-done.3
  63.9 0.9 copy-done.5
  64.9 0.9 copy-done.7
  65.8 0.9 copy-done.9
  66.7 2.0 %shard_map.68.kern_ref = bf16[1024,512]{1,0:T(8,128)(2,1)S(1)} custom-call(s32[1]{0:T(128)} %bitcast.land_ref, bf16[256,1280]{1,0:T(8,128)(2,1)S(1)} %copy-done.1, bf16[256,1280]{1,0:T(8,128)(2,1)S(1)} %collective-permute-done.refs_1_, bf16[256,1280]{1,0:T(8,128)(2,1)S(1)} %collective-permute-done.1.refs_2_, ...), custom_call_target="tpu_custom_call" | custom-call | flops 1342177280 | bytes 4980736 | tf_op jit(solution)/shard_map/pallas_call | solution.py:42
  68.7 0.0 copy-start.10
  68.8 2.3 %collective-permute-done.14.refs_5_ = bf16[64,1024]{1,0:T(8,128)(2,1)S(1)} collective-permute-done((bf16[64,1024]{1,0:T(8,128)(2,1)S(1)}, bf16[64,1024]{1,0:T(8,128)(2,1)S(1)}, u32[]{:S(2)}, u32[]{:S(2)}) %collective-permute-start.14) | collective-permute-done | bytes 131104 | tf_op jit(solution)/shard_map/ppermute | solution.py:183
  71.0 0.7 shard_map.69
  71.8 1.4 %collective-permute-start.17 = (bf16[512,512]{1,0:T(8,128)(2,1)S(1)}, bf16[512,512]{1,0:T(8,128)(2,1)S(1)}, u32[]{:S(2)}, u32[]{:S(2)}) collective-permute-start(bf16[512,512]{1,0:T(8,128)(2,1)S(1)} %get-tuple-element.15), channel_id=1, source_target_pairs={{0,1},{1,0},{2,3},{3,2},{4,5},{5,4},{6,7},{7,6},{8,9},{9,8},{10,11... | collective-permute-start | bytes 1572872 | tf_op jit(solution)/shard_map/ppermute | solution.py:183
  73.2 0.7 shard_map.72
  73.9 0.1 collective-permute-start.19
  74.0 0.2 convert_reduce_fusion
  74.3 0.4 collective-permute-done.17.refs_1_
  74.7 0.1 shard_map.70
  74.8 1.3 collective-permute-start.18
  76.1 0.4 select_reduce_fusion
  76.4 0.7 all_to_all.9
  77.1 6.1 %all-to-all-start = ((s32[32,1,32]{2,1,0:T(1,128)}), s32[32,1,32]{2,1,0:T(1,128)S(1)}, u32[]{:S(2)}, u32[]{:S(2)}) async-start(s32[32,1,32]{2,1,0:T(1,128)} %all_to_all.9), calls=%async_computation | async-start | bytes 32768 | tf_op jit(solution)/shard_map/all_to_all | solution.py:243
  83.2 0.1 shard_map.73
  83.3 1.2 collective-permute-start.20
  84.6 0.4 fusion.refs_2_.refs_3_
  85.0 0.5 shard_map.71
  85.5 5.6 %collective-permute-done.20.refs_1_ = bf16[512,256]{1,0:T(8,128)(2,1)S(1)} collective-permute-done((bf16[512,256]{1,0:T(8,128)(2,1)S(1)}, bf16[512,256]{1,0:T(8,128)(2,1)S(1)}, u32[]{:S(2)}, u32[]{:S(2)}) %collective-permute-start.20) | collective-permute-done | bytes 262176 | tf_op jit(solution)/shard_map/ppermute | solution.py:186
  91.0 1.5 %shard_map.74 = (bf16[512,256]{1,0:T(8,128)(2,1)S(1)}, bf16[1024,512]{1,0:T(8,128)(2,1)}) custom-call(s32[1]{0:T(128)} %bitcast.land_ref, bf16[512,256]{1,0:T(8,128)(2,1)S(1)} %get-tuple-element.21.refs_0_, bf16[512,256]{1,0:T(8,128)(2,1)S(1)} %collective-permute-done.20.refs_1_, bf16[1024,256]{1,0:T(8,128)(2,1)S(1)} %get-tuple-element.23.refs_2_, ...), custom_call_target="tpu_custom_call" | custom-call | flops 268435456 | bytes 3407872 | tf_op jit(solution)/shard_map/pallas_call | solution.py:42
  92.5 6.5 %all-to-all-start.1 = ((bf16[32,32,512]{2,1,0:T(8,128)(2,1)}), bf16[32,32,512]{2,1,0:T(8,128)(2,1)S(1)}, u32[]{:S(2)}, u32[]{:S(2)}) async-start(bf16[32,32,512]{2,1,0:T(8,128)(2,1)} %bitcast.1), calls=%async_computation.1 | async-start | bytes 2097152 | tf_op jit(solution)/shard_map/all_to_all | solution.py:259
  99.0 1.2 collective-permute-start.22
  100.3 0.3 collective-permute-start.21
  100.5 0.5 broadcast.31
  101.1 0.7 reduce.3
  101.7 0.1 reshape.26.ids_ref
  101.8 12.0 %collective-permute-done.22.refs_3_ = bf16[512,256]{1,0:T(8,128)(2,1)S(1)} collective-permute-done((bf16[512,256]{1,0:T(8,128)(2,1)S(1)}, bf16[512,256]{1,0:T(8,128)(2,1)S(1)}, u32[]{:S(2)}, u32[]{:S(2)}) %collective-permute-start.22) | collective-permute-done | bytes 262176 | tf_op jit(solution)/shard_map/ppermute | solution.py:186
  113.8 9.3 %collective-permute-done.21.refs_2_ = bf16[512,256]{1,0:T(8,128)(2,1)S(1)} collective-permute-done((bf16[512,256]{1,0:T(8,128)(2,1)S(1)}, bf16[512,256]{1,0:T(8,128)(2,1)S(1)}, u32[]{:S(2)}, u32[]{:S(2)}) %collective-permute-start.21) | collective-permute-done | bytes 262176 | tf_op jit(solution)/shard_map/ppermute | solution.py:186
  123.1 2.2 %copy-done = bf16[2048,1024]{1,0:T(8,128)(2,1)S(1)} copy-done((bf16[2048,1024]{1,0:T(8,128)(2,1)S(1)}, bf16[2048,1024]{1,0:T(8,128)(2,1)}, u32[]{:S(2)}) %copy-start) | copy-done | bytes 4194328
  125.3 6.3 %distances.1 = f32[512,2048]{1,0:T(8,128)} custom-call(s32[1]{0:T(128)} %bitcast.land_ref, bf16[512,256]{1,0:T(8,128)(2,1)S(1)} %get-tuple-element.18.refs_0_, bf16[512,256]{1,0:T(8,128)(2,1)S(1)} %get-tuple-element.24.refs_1_, bf16[512,256]{1,0:T(8,128)(2,1)S(1)} %collective-permute-done.21.refs_2_, bf16[512,256]{1,0:T(8,128)(2,1)S(1)} %collective-permute-done.22.refs_3_, ...), custom_call_target="tpu_custom_call" | custom-call | flops 2147483648 | bytes 8388608 | tf_op jit(solution)/shard_map/distances/pallas_call | solution.py:271
  131.6 1.1 shard_map.75
  (26 shorter events, 0.1 us)
Async XLA Ops:
  0.6 15.9 %collective-permute-start = (bf16[256,1280]{1,0:T(8,128)(2,1)}, bf16[256,1280]{1,0:T(8,128)(2,1)S(1)}, u32[]{:S(2)}, u32[]{:S(2)}) collective-permute-start(bf16[256,1280]{1,0:T(8,128)(2,1)} %refs_0_.3), channel_id=1, source_target_pairs={{0,16},{16,0},{1,17},{17,1},{2,18},{18,2},{3,19},{19,3},{4,20},{20... | collective-permute-start | bytes 1966088 | tf_op jit(solution)/shard_map/ppermute | solution.py:186
  1.9 59.8 %collective-permute-start.1 = (bf16[256,1280]{1,0:T(8,128)(2,1)}, bf16[256,1280]{1,0:T(8,128)(2,1)S(1)}, u32[]{:S(2)}, u32[]{:S(2)}) collective-permute-start(bf16[256,1280]{1,0:T(8,128)(2,1)} %refs_0_.3), channel_id=1, source_target_pairs={{0,1},{1,0},{2,3},{3,2},{4,5},{5,4},{6,7},{7,6},{8,9},{9,8},{10,11... | collective-permute-start | bytes 1966088 | tf_op jit(solution)/shard_map/ppermute | solution.py:183
  16.5 45.4 %collective-permute-start.2 = (bf16[256,1280]{1,0:T(8,128)(2,1)S(1)}, bf16[256,1280]{1,0:T(8,128)(2,1)S(1)}, u32[]{:S(2)}, u32[]{:S(2)}) collective-permute-start(bf16[256,1280]{1,0:T(8,128)(2,1)S(1)} %collective-permute-done.refs_1_), channel_id=1, source_target_pairs={{0,1},{1,0},{2,3},{3,2},{4,5},{5,4},{6,7},{7,6},{8,9},{9,8},{10,11... | collective-permute-start | bytes 1966088 | tf_op jit(solution)/shard_map/ppermute | solution.py:183
  18.1 14.4 %collective-permute-start.12 = (bf16[64,1024]{1,0:T(8,128)(2,1)}, bf16[64,1024]{1,0:T(8,128)(2,1)S(1)}, u32[]{:S(2)}, u32[]{:S(2)}) collective-permute-start(bf16[64,1024]{1,0:T(8,128)(2,1)} %refs_0_.5), channel_id=1, source_target_pairs={{0,12},{1,13},{2,14},{3,15},{4,8},{5,9},{6,10},{7,11},{8,4},{9,5},... | collective-permute-start | bytes 393224 | tf_op jit(solution)/shard_map/ppermute | solution.py:183
  19.4 21.7 %collective-permute-start.5 = (bf16[64,1280]{1,0:T(8,128)(2,1)}, bf16[64,1280]{1,0:T(8,128)(2,1)S(1)}, u32[]{:S(2)}, u32[]{:S(2)}) collective-permute-start(bf16[64,1280]{1,0:T(8,128)(2,1)} %refs_4_.2), channel_id=1, source_target_pairs={{0,12},{1,13},{2,14},{3,15},{4,8},{5,9},{6,10},{7,11},{8,4},{9,5},... | collective-permute-start | bytes 491528 | tf_op jit(solution)/shard_map/ppermute | solution.py:183
  19.5 18.5 %collective-permute-start.11 = (bf16[64,1024]{1,0:T(8,128)(2,1)}, bf16[64,1024]{1,0:T(8,128)(2,1)S(1)}, u32[]{:S(2)}, u32[]{:S(2)}) collective-permute-start(bf16[64,1024]{1,0:T(8,128)(2,1)} %refs_0_.5), channel_id=1, source_target_pairs={{0,8},{1,9},{2,10},{3,11},{4,12},{5,13},{6,14},{7,15},{8,0},{9,1},... | collective-permute-start | bytes 393224 | tf_op jit(solution)/shard_map/ppermute | solution.py:183
  32.4 8.6 %collective-permute-start.10 = (bf16[64,1024]{1,0:T(8,128)(2,1)}, bf16[64,1024]{1,0:T(8,128)(2,1)S(1)}, u32[]{:S(2)}, u32[]{:S(2)}) collective-permute-start(bf16[64,1024]{1,0:T(8,128)(2,1)} %refs_0_.5), channel_id=1, source_target_pairs={{0,4},{1,5},{2,6},{3,7},{4,0},{5,1},{6,2},{7,3},{8,12},{9,13},{10,... | collective-permute-start | bytes 393224 | tf_op jit(solution)/shard_map/ppermute | solution.py:183
  38.0 9.5 %collective-permute-start.4 = (bf16[64,1280]{1,0:T(8,128)(2,1)}, bf16[64,1280]{1,0:T(8,128)(2,1)S(1)}, u32[]{:S(2)}, u32[]{:S(2)}) collective-permute-start(bf16[64,1280]{1,0:T(8,128)(2,1)} %refs_4_.2), channel_id=1, source_target_pairs={{0,8},{1,9},{2,10},{3,11},{4,12},{5,13},{6,14},{7,15},{8,0},{9,1},... | collective-permute-start | bytes 491528 | tf_op jit(solution)/shard_map/ppermute | solution.py:183
  41.0 7.7 %collective-permute-start.3 = (bf16[64,1280]{1,0:T(8,128)(2,1)}, bf16[64,1280]{1,0:T(8,128)(2,1)S(1)}, u32[]{:S(2)}, u32[]{:S(2)}) collective-permute-start(bf16[64,1280]{1,0:T(8,128)(2,1)} %refs_4_.2), channel_id=1, source_target_pairs={{0,4},{1,5},{2,6},{3,7},{4,0},{5,1},{6,2},{7,3},{8,12},{9,13},{10,... | collective-permute-start | bytes 491528 | tf_op jit(solution)/shard_map/ppermute | solution.py:183
  41.0 8.0 %collective-permute-start.6 = (bf16[64,1280]{1,0:T(8,128)(2,1)}, bf16[64,1280]{1,0:T(8,128)(2,1)S(1)}, u32[]{:S(2)}, u32[]{:S(2)}) collective-permute-start(bf16[64,1280]{1,0:T(8,128)(2,1)} %refs_4_.2), channel_id=1, source_target_pairs={{0,2},{1,3},{2,0},{3,1},{4,6},{5,7},{6,4},{7,5},{8,10},{9,11},{10,... | collective-permute-start | bytes 491528 | tf_op jit(solution)/shard_map/ppermute | solution.py:183
  47.5 5.3 %collective-permute-start.9 = (bf16[64,1280]{1,0:T(8,128)(2,1)S(1)}, bf16[64,1280]{1,0:T(8,128)(2,1)S(1)}, u32[]{:S(2)}, u32[]{:S(2)}) collective-permute-start(bf16[64,1280]{1,0:T(8,128)(2,1)S(1)} %collective-permute-done.5.refs_7_), channel_id=1, source_target_pairs={{0,2},{1,3},{2,0},{3,1},{4,6},{5,7},{6,4},{7,5},{8,10},{9,11},{10,... | collective-permute-start | bytes 491528 | tf_op jit(solution)/shard_map/ppermute | solution.py:183
  48.7 7.5 %collective-permute-start.8 = (bf16[64,1280]{1,0:T(8,128)(2,1)S(1)}, bf16[64,1280]{1,0:T(8,128)(2,1)S(1)}, u32[]{:S(2)}, u32[]{:S(2)}) collective-permute-start(bf16[64,1280]{1,0:T(8,128)(2,1)S(1)} %collective-permute-done.4.refs_6_), channel_id=1, source_target_pairs={{0,2},{1,3},{2,0},{3,1},{4,6},{5,7},{6,4},{7,5},{8,10},{9,11},{10,... | collective-permute-start | bytes 491528 | tf_op jit(solution)/shard_map/ppermute | solution.py:183
  49.0 10.8 %collective-permute-start.7 = (bf16[64,1280]{1,0:T(8,128)(2,1)S(1)}, bf16[64,1280]{1,0:T(8,128)(2,1)S(1)}, u32[]{:S(2)}, u32[]{:S(2)}) collective-permute-start(bf16[64,1280]{1,0:T(8,128)(2,1)S(1)} %collective-permute-done.3.refs_5_), channel_id=1, source_target_pairs={{0,2},{1,3},{2,0},{3,1},{4,6},{5,7},{6,4},{7,5},{8,10},{9,11},{10,... | collective-permute-start | bytes 491528 | tf_op jit(solution)/shard_map/ppermute | solution.py:183
  52.8 0.7 copy-start.4
  53.4 15.3 %collective-permute-start.13 = (bf16[64,1024]{1,0:T(8,128)(2,1)}, bf16[64,1024]{1,0:T(8,128)(2,1)S(1)}, u32[]{:S(2)}, u32[]{:S(2)}) collective-permute-start(bf16[64,1024]{1,0:T(8,128)(2,1)} %refs_0_.5), channel_id=1, source_target_pairs={{0,2},{1,3},{2,0},{3,1},{4,6},{5,7},{6,4},{7,5},{8,10},{9,11},{10,... | collective-permute-start | bytes 393224 | tf_op jit(solution)/shard_map/ppermute | solution.py:183
  56.3 0.7 copy-start.6
  57.0 11.8 %collective-permute-start.16 = (bf16[64,1024]{1,0:T(8,128)(2,1)S(1)}, bf16[64,1024]{1,0:T(8,128)(2,1)S(1)}, u32[]{:S(2)}, u32[]{:S(2)}) collective-permute-start(bf16[64,1024]{1,0:T(8,128)(2,1)S(1)} %collective-permute-done.12.refs_3_), channel_id=1, source_target_pairs={{0,2},{1,3},{2,0},{3,1},{4,6},{5,7},{6,4},{7,5},{8,10},{9,11},{10,... | collective-permute-start | bytes 393224 | tf_op jit(solution)/shard_map/ppermute | solution.py:183
  59.8 0.7 copy-start.8
  60.5 8.3 %collective-permute-start.15 = (bf16[64,1024]{1,0:T(8,128)(2,1)S(1)}, bf16[64,1024]{1,0:T(8,128)(2,1)S(1)}, u32[]{:S(2)}, u32[]{:S(2)}) collective-permute-start(bf16[64,1024]{1,0:T(8,128)(2,1)S(1)} %collective-permute-done.11.refs_2_), channel_id=1, source_target_pairs={{0,2},{1,3},{2,0},{3,1},{4,6},{5,7},{6,4},{7,5},{8,10},{9,11},{10,... | collective-permute-start | bytes 393224 | tf_op jit(solution)/shard_map/ppermute | solution.py:183
  61.7 9.3 %collective-permute-start.14 = (bf16[64,1024]{1,0:T(8,128)(2,1)S(1)}, bf16[64,1024]{1,0:T(8,128)(2,1)S(1)}, u32[]{:S(2)}, u32[]{:S(2)}) collective-permute-start(bf16[64,1024]{1,0:T(8,128)(2,1)S(1)} %collective-permute-done.10.refs_1_), channel_id=1, source_target_pairs={{0,2},{1,3},{2,0},{3,1},{4,6},{5,7},{6,4},{7,5},{8,10},{9,11},{10,... | collective-permute-start | bytes 393224 | tf_op jit(solution)/shard_map/ppermute | solution.py:183
  61.9 1.1 copy-start.1
  63.0 0.9 copy-start.3
  63.9 0.9 copy-start.5
  64.9 0.9 copy-start.7
  65.8 0.9 copy-start.9
  66.7 4.3 %copy-start.2 = (bf16[64,1024]{1,0:T(8,128)(2,1)S(1)}, bf16[64,1024]{1,0:T(8,128)(2,1)}, u32[]{:S(2)}) copy-start(bf16[64,1024]{1,0:T(8,128)(2,1)} %refs_0_.5) | copy-start | bytes 393220
  68.7 4.5 %copy-start.10 = (s32[512]{0:T(512)S(1)}, s32[512]{0:T(512)}, u32[]{:S(2)}) copy-start(s32[512]{0:T(512)} %param.9) | copy-start | bytes 6148
  71.8 3.0 %collective-permute-start.17 = (bf16[512,512]{1,0:T(8,128)(2,1)S(1)}, bf16[512,512]{1,0:T(8,128)(2,1)S(1)}, u32[]{:S(2)}, u32[]{:S(2)}) collective-permute-start(bf16[512,512]{1,0:T(8,128)(2,1)S(1)} %get-tuple-element.15), channel_id=1, source_target_pairs={{0,1},{1,0},{2,3},{3,2},{4,5},{5,4},{6,7},{7,6},{8,9},{9,8},{10,11... | collective-permute-start | bytes 1572872 | tf_op jit(solution)/shard_map/ppermute | solution.py:183
  73.9 9.3 %collective-permute-start.19 = (bf16[512,512]{1,0:T(8,128)(2,1)S(1)}, bf16[512,512]{1,0:T(8,128)(2,1)S(1)}, u32[]{:S(2)}, u32[]{:S(2)}) collective-permute-start(bf16[512,512]{1,0:T(8,128)(2,1)S(1)} %get-tuple-element.20), channel_id=1, source_target_pairs={{0,1},{1,0},{2,3},{3,2},{4,5},{5,4},{6,7},{7,6},{8,9},{9,8},{10,11... | collective-permute-start | bytes 1572872 | tf_op jit(solution)/shard_map/ppermute | solution.py:183
  74.8 10.2 %collective-permute-start.18 = (bf16[512,256]{1,0:T(8,128)(2,1)S(1)}, bf16[512,256]{1,0:T(8,128)(2,1)S(1)}, u32[]{:S(2)}, u32[]{:S(2)}) collective-permute-start(bf16[512,256]{1,0:T(8,128)(2,1)S(1)} %get-tuple-element.17), channel_id=1, source_target_pairs={{0,16},{16,0},{1,17},{17,1},{2,18},{18,2},{3,19},{19,3},{4,20},{20... | collective-permute-start | bytes 786440 | tf_op jit(solution)/shard_map/ppermute | solution.py:186
  77.1 15.4 %all-to-all-start = ((s32[32,1,32]{2,1,0:T(1,128)}), s32[32,1,32]{2,1,0:T(1,128)S(1)}, u32[]{:S(2)}, u32[]{:S(2)}) async-start(s32[32,1,32]{2,1,0:T(1,128)} %all_to_all.9), calls=%async_computation | async-start | bytes 32768 | tf_op jit(solution)/shard_map/all_to_all | solution.py:243
  83.3 7.7 %collective-permute-start.20 = (bf16[512,256]{1,0:T(8,128)(2,1)S(1)}, bf16[512,256]{1,0:T(8,128)(2,1)S(1)}, u32[]{:S(2)}, u32[]{:S(2)}) collective-permute-start(bf16[512,256]{1,0:T(8,128)(2,1)S(1)} %get-tuple-element.22), channel_id=1, source_target_pairs={{0,16},{16,0},{1,17},{17,1},{2,18},{18,2},{3,19},{19,3},{4,20},{20... | collective-permute-start | bytes 786440 | tf_op jit(solution)/shard_map/ppermute | solution.py:186
  92.5 39.1 %all-to-all-start.1 = ((bf16[32,32,512]{2,1,0:T(8,128)(2,1)}), bf16[32,32,512]{2,1,0:T(8,128)(2,1)S(1)}, u32[]{:S(2)}, u32[]{:S(2)}) async-start(bf16[32,32,512]{2,1,0:T(8,128)(2,1)} %bitcast.1), calls=%async_computation.1 | async-start | bytes 2097152 | tf_op jit(solution)/shard_map/all_to_all | solution.py:259
  99.0 14.8 %collective-permute-start.22 = (bf16[512,256]{1,0:T(8,128)(2,1)S(1)}, bf16[512,256]{1,0:T(8,128)(2,1)S(1)}, u32[]{:S(2)}, u32[]{:S(2)}) collective-permute-start(bf16[512,256]{1,0:T(8,128)(2,1)S(1)} %get-tuple-element.24.refs_1_), channel_id=1, source_target_pairs={{0,16},{16,0},{1,17},{17,1},{2,18},{18,2},{3,19},{19,3},{4,20},{20... | collective-permute-start | bytes 786440 | tf_op jit(solution)/shard_map/ppermute | solution.py:186
  100.3 22.8 %collective-permute-start.21 = (bf16[512,256]{1,0:T(8,128)(2,1)S(1)}, bf16[512,256]{1,0:T(8,128)(2,1)S(1)}, u32[]{:S(2)}, u32[]{:S(2)}) collective-permute-start(bf16[512,256]{1,0:T(8,128)(2,1)S(1)} %get-tuple-element.18.refs_0_), channel_id=1, source_target_pairs={{0,16},{16,0},{1,17},{17,1},{2,18},{18,2},{3,19},{19,3},{4,20},{20... | collective-permute-start | bytes 786440 | tf_op jit(solution)/shard_map/ppermute | solution.py:186
  123.1 2.2 %copy-start = (bf16[2048,1024]{1,0:T(8,128)(2,1)S(1)}, bf16[2048,1024]{1,0:T(8,128)(2,1)}, u32[]{:S(2)}) copy-start(bf16[2048,1024]{1,0:T(8,128)(2,1)} %refs_4_.3) | copy-start | bytes 12582916
where the time goes:
time: 134 us; the launch traced here: 133 us
  waiting for transfers between devices  68.6 us (51%)
  starting transfers between devices  38.4 us (29%)
  Pallas kernels  13 us (10%)
  local copies, waits for them, and re-layouts  10.2 us (8%)
  other arithmetic  1.72 us (1%)
    ppermute x5, waiting for transfers between devices, land_send(): lax.ppermute(x, 'land', [(s, (s + step) % land_count) for s in range(land...  40.5 us
    ppermute x18, waiting for transfers between devices, move(): return lax.ppermute(x, 'dp', axis_perm(sizes, axis, step))  28.1 us
    ppermute x18, starting transfers between devices, move(): return lax.ppermute(x, 'dp', axis_perm(sizes, axis, step))  20.5 us
    unnamed x22, local copies, waits for them, and re-layouts  8.95 us
    pallas_call x8, Pallas kernels, call(): pl.pallas_call(body, out_shape=list(outs), in_specs=[SMEM] + [VMEM] * len...  6.67 us
    all_to_all x1, starting transfers between devices, local(): lax.all_to_all(outgoing.reshape(land_count * dp_count, slot_count, keep_w...  6.5 us
    pallas_call x1, Pallas kernels, local(): pl.pallas_call(functools.partial(distance_body, land_count, parts), grid=...  6.31 us
    all_to_all x1, starting transfers between devices, local(): lax.all_to_all(slot_ids.reshape(land_count * dp_count, slot_count), every...  6.06 us
  transfers between devices with their start and end apart: 25, of which 12 were waited for; matrix products, arithmetic and copies ran while one was open for 2% of the time, Pallas kernels for 8%

commit v1 on v0

--- a/solution.py
+++ b/solution.py
@@ -53,6 +53,11 @@
 def column_to_row(column):
     wide = jnp.broadcast_to(column, (column.shape[0], 128))
     return jnp.transpose(wide)[0:1]
+
+
+def stage_body(land_ref, *refs):
+    for src, out in zip(refs[: len(refs) // 2], refs[len(refs) // 2 :]):
+        out[...] = src[...]
 
 
 def kernel_body(land_count, cores, pieces, land_ref, *refs):
@@ -119,33 +124,48 @@
     out_ref[:, start:] = value.astype(out_ref.dtype)
 
 
-def distance_body(land_count, parts, land_ref, *refs):
-    count = land_count * parts
-    feats, cent_ref, out_ref, feat_sq = refs[:count], refs[count], refs[count + 1], refs[count + 2]
+def square_sum(parts):
+    total = None
+    for part in parts:
+        term = jnp.sum(jnp.square(part[...].astype(jnp.float32)), axis=1, keepdims=True)
+        total = term if total is None else total + term
+    return total
+
+
+def cross_sum(feats, cent_ref, first, land_count, parts, land_ref):
+    width = feats[0].shape[1]
+    cross = None
+    for i, feat in enumerate(feats):
+        source = lax.rem(land_ref[0] + first + i // parts, land_count)
+        columns = pl.ds(pl.multiple_of((source * parts + i % parts) * width, 128), width)
+        term = lax.dot_general(
+            feat[...], cent_ref[:, columns], (((1,), (1,)), ((), ())), preferred_element_type=jnp.float32
+        )
+        cross = term if cross is None else cross + term
+    return cross
+
+
+def near_body(land_count, parts, land_ref, *refs):
+    *feats, cent_ref, out_ref, feat_sq = refs
 
     @pl.when(pl.program_id(0) == 0)
     def _():
-        total = jnp.zeros(feat_sq.shape, jnp.float32)
-        for feat in feats:
-            total = total + jnp.sum(jnp.square(feat[...].astype(jnp.float32)), axis=1, keepdims=True)
-        feat_sq[...] = total
-
-    cent = cent_ref[...]
-    cent_sq = column_to_row(jnp.sum(jnp.square(cent.astype(jnp.float32)), axis=1, keepdims=True))
-    width = feats[0].shape[1]
-    cross = None
-    for s in range(land_count):
-        source = lax.rem(land_ref[0] + s, land_count)
-        for h in range(parts):
-            columns = pl.ds(pl.multiple_of((source * parts + h) * width, 128), width)
-            term = lax.dot_general(
-                feats[s * parts + h][...],
-                cent_ref[:, columns],
-                (((1,), (1,)), ((), ())),
-                preferred_element_type=jnp.float32,
-            )
-            cross = term if cross is None else cross + term
-    out_ref[...] = (feat_sq[...] + cent_sq - 2.0 * cross) / cent_ref.shape[1]
+        feat_sq[...] = square_sum(feats)
+
+    cent_sq = column_to_row(jnp.sum(jnp.square(cent_ref[...].astype(jnp.float32)), axis=1, keepdims=True))
+    cross = cross_sum(feats, cent_ref, 0, land_count, parts, land_ref)
+    out_ref[...] = feat_sq[...] + cent_sq - 2.0 * cross
+
+
+def distance_body(land_count, parts, land_ref, *refs):
+    *feats, cent_ref, near_ref, out_ref, feat_sq = refs
+
+    @pl.when(pl.program_id(0) == 0)
+    def _():
+        feat_sq[...] = square_sum(feats)
+
+    cross = cross_sum(feats, cent_ref, 1, land_count, parts, land_ref)
+    out_ref[...] = (near_ref[...] + feat_sq[...] - 2.0 * cross) / cent_ref.shape[1]
 
 
 def mean_body(land_count, land_ref, ids_ref, arrived_ref, out_ref):
@@ -185,22 +205,42 @@
     def land_send(x, step):
         return lax.ppermute(x, "land", [(s, (s + step) % land_count) for s in range(land_count)])
 
-    def outer_shifts(x):
-        return [x] + [move(x, 0, k) for k in range(1, sizes[0])]
-
-    def middle_shifts(pieces):
-        return pieces + [move(p, 1, k) for p in pieces for k in range(1, sizes[1])]
+    def along_z(x):
+        pieces = [x]
+        for k in range(1, sizes[0]):
+            relayed = sizes[0] == 4 and k == 3
+            pieces.append(move(pieces[2] if relayed else x, 0, 1 if relayed else k))
+        return pieces
+
+    def along_y(pieces, relay):
+        out = list(pieces)
+        for k in range(1, sizes[1]):
+            first = move(pieces[0], 1, k)
+            for i, piece in enumerate(pieces):
+                if i == 0:
+                    out.append(first)
+                elif i == 1 and relay:
+                    out.append(move(first, 0, 1))
+                else:
+                    out.append(move(piece, 1, k))
+        return out
 
     row_pieces = [embeddings] + [land_send(embeddings, land_count - k) for k in range(1, land_count)]
     row_pieces = row_pieces + [move(p, 2, k) for k in range(1, cores) for p in row_pieces]
-    marks = middle_shifts(outer_shifts(landmarks))
+    marks = along_y(along_z(landmarks), False)
     parts = factor_parts(feat_width, land_count)
     keep_width = feat_width // land_count
     width = keep_width // parts
-    factors = middle_shifts(outer_shifts(factor))
+    factors = along_y(along_z(factor), sizes[0] > 1)
 
     rows_all = group_rows * cores
     depth_all = landmarks.shape[0] * len(marks)
+    row_pieces[0], marks[0], factors[0] = call(
+        stage_body,
+        [shape(*a.shape, a.dtype) for a in (embeddings, landmarks, factor)],
+        [embeddings, landmarks, factor],
+        land,
+    )
     (kern,) = call(
         functools.partial(kernel_body, land_count, cores, len(marks)),
         [shape(rows_all, depth_all, bf16)],
@@ -264,27 +304,33 @@
         tiled=True,
     )
     arrived = arrived.reshape(slot_total, keep_width)
-    feats = mine + [land_send(mine[h], land_count - s) for s in range(1, land_count) for h in range(parts)]
+    others = [land_send(mine[h], land_count - s) for s in range(1, land_count) for h in range(parts)]
 
     cent_block = centroids.shape[0]
     block = min(256, cent_block)
-    distances = pl.pallas_call(
-        functools.partial(distance_body, land_count, parts),
-        grid=(cent_block // block,),
-        out_shape=shape(group_rows, cent_block, f32),
-        in_specs=[SMEM]
-        + [pl.BlockSpec((group_rows, width), lambda i: (0, 0))] * len(feats)
-        + [pl.BlockSpec((block, feat_width), lambda i: (i, 0))],
-        out_specs=pl.BlockSpec((group_rows, block), lambda i: (0, i)),
-        scratch_shapes=[pltpu.VMEM((group_rows, 1), f32)],
-        cost_estimate=pl.CostEstimate(
-            flops=2 * group_rows * cent_block * feat_width,
-            bytes_accessed=2 * cent_block * feat_width + 4 * group_rows * cent_block,
-            transcendentals=0,
-        ),
-        compiler_params=pltpu.CompilerParams(vmem_limit_bytes=24 * 2**20),
-        name="distances",
-    )(land, *feats, centroids)
+
+    def by_block(body, feats, more):
+        tile = pl.BlockSpec((group_rows, block), lambda i: (0, i))
+        return pl.pallas_call(
+            functools.partial(body, land_count, parts),
+            grid=(cent_block // block,),
+            out_shape=shape(group_rows, cent_block, f32),
+            in_specs=[SMEM]
+            + [pl.BlockSpec((group_rows, width), lambda i: (0, 0))] * len(feats)
+            + [pl.BlockSpec((block, feat_width), lambda i: (i, 0))]
+            + [tile] * len(more),
+            out_specs=tile,
+            scratch_shapes=[pltpu.VMEM((group_rows, 1), f32)],
+            cost_estimate=pl.CostEstimate(
+                flops=2 * group_rows * cent_block * width * len(feats),
+                bytes_accessed=2 * cent_block * feat_width + 4 * group_rows * cent_block * (1 + len(more)),
+                transcendentals=0,
+            ),
+            compiler_params=pltpu.CompilerParams(vmem_limit_bytes=16 * 2**20),
+        )(land, *feats, centroids, *more)
+
+    near = by_block(near_body, mine, [])
+    distances = by_block(distance_body, others, [near])
     (new_centroids,) = call(
         functools.partial(mean_body, land_count),
         [shape(own_width, feat_width, f32)],

time: 134 us -> 124 us (0.925)
  waiting for transfers between devices: 68.6 us -> 61.1 us
  starting transfers between devices: 38.4 us -> 31.2 us
  Pallas kernels: 13 us -> 16 us
    ppermute x18, starting transfers between devices: 20.5 us -> 13.7 us  [move(): return lax.ppermute(x, 'dp', axis_perm(sizes, axis, step))]
    ppermute x5, waiting for transfers between devices: 40.5 us -> 34.4 us  [land_send(): lax.ppermute(x, 'land', [(s, (s + step) % land_count) for s in range(land...]
    pallas_call x1 -> x2, Pallas kernels: 6.31 us -> 9.23 us  [by_block(): pl.pallas_call(functools.partial(body, land_count, parts), grid=(cent_blo...]
    ppermute x18, waiting for transfers between devices: 28.1 us -> 26.7 us  [move(): return lax.ppermute(x, 'dp', axis_perm(sizes, axis, step))]
    unnamed x22 -> x24, local copies, waits for them, and re-layouts: 8.95 us -> 9.83 us
    pallas_call x8 -> x9, Pallas kernels: 6.67 us -> 6.73 us  [call(): pl.pallas_call(body, out_shape=list(outs), in_specs=[SMEM] + [VMEM] * len...]
  transfers between devices with their start and end apart: 25 -> 25, of which waited for: 12 -> 12; matrix products, arithmetic and copies ran while one was open for 2% -> 2% of each run, Pallas kernels for 8% -> 12%
where the time goes in v1:
time: 124 us; the launch traced here: 122 us
  waiting for transfers between devices  61.1 us (49%)
  starting transfers between devices  31.2 us (25%)
  Pallas kernels  16 us (13%)
  local copies, waits for them, and re-layouts  11.1 us (9%)
  other arithmetic  1.72 us (1%)
    ppermute x5, waiting for transfers between devices, land_send(): lax.ppermute(x, 'land', [(s, (s + step) % land_count) for s in range(land...  34.4 us
    ppermute x18, waiting for transfers between devices, move(): return lax.ppermute(x, 'dp', axis_perm(sizes, axis, step))  26.7 us
    ppermute x18, starting transfers between devices, move(): return lax.ppermute(x, 'dp', axis_perm(sizes, axis, step))  13.7 us
    unnamed x24, local copies, waits for them, and re-layouts  9.83 us
    pallas_call x2, Pallas kernels, by_block(): pl.pallas_call(functools.partial(body, land_count, parts), grid=(cent_blo...  9.23 us
    pallas_call x9, Pallas kernels, call(): pl.pallas_call(body, out_shape=list(outs), in_specs=[SMEM] + [VMEM] * len...  6.73 us
    all_to_all x1, starting transfers between devices, local(): lax.all_to_all(outgoing.reshape(land_count * dp_count, slot_count, keep_w...  6.5 us
    all_to_all x1, starting transfers between devices, local(): lax.all_to_all(slot_ids.reshape(land_count * dp_count, slot_count), every...  5.72 us
  transfers between devices with their start and end apart: 25, of which 12 were waited for; matrix products, arithmetic and copies ran while one was open for 2% of the time, Pallas kernels for 12%

profile of v1, /device:TPU:9, one launch (start us, length us, event | category | flops | bytes accessed | tf_op | source)
XLA Modules:
  0.0 121.9 jit_solution(9995935929485952134)
XLA Ops:
  0.6 1.3 %collective-permute-start = (bf16[256,1280]{1,0:T(8,128)(2,1)}, bf16[256,1280]{1,0:T(8,128)(2,1)S(1)}, u32[]{:S(2)}, u32[]{:S(2)}) collective-permute-start(bf16[256,1280]{1,0:T(8,128)(2,1)} %refs_0_.1), channel_id=1, source_target_pairs={{0,16},{16,0},{1,17},{17,1},{2,18},{18,2},{3,19},{19,3},{4,20},{20... | collective-permute-start | bytes 1966088 | tf_op jit(solution)/shard_map/ppermute | solution.py:206
  1.9 1.0 collective-permute-start.1
  2.9 13.7 %collective-permute-done.refs_1_ = bf16[256,1280]{1,0:T(8,128)(2,1)S(1)} collective-permute-done((bf16[256,1280]{1,0:T(8,128)(2,1)}, bf16[256,1280]{1,0:T(8,128)(2,1)S(1)}, u32[]{:S(2)}, u32[]{:S(2)}) %collective-permute-start) | collective-permute-done | bytes 655392 | tf_op jit(solution)/shard_map/ppermute | solution.py:206
  16.5 1.5 %collective-permute-start.2 = (bf16[256,1280]{1,0:T(8,128)(2,1)S(1)}, bf16[256,1280]{1,0:T(8,128)(2,1)S(1)}, u32[]{:S(2)}, u32[]{:S(2)}) collective-permute-start(bf16[256,1280]{1,0:T(8,128)(2,1)S(1)} %collective-permute-done.refs_1_), channel_id=1, source_target_pairs={{0,1},{1,0},{2,3},{3,2},{4,5},{5,4},{6,7},{7,6},{8,9},{9,8},{10,11... | collective-permute-start | bytes 1966088 | tf_op jit(solution)/shard_map/ppermute | solution.py:203
  18.1 1.2 %collective-permute-start.13 = (bf16[64,1024]{1,0:T(8,128)(2,1)}, bf16[64,1024]{1,0:T(8,128)(2,1)S(1)}, u32[]{:S(2)}, u32[]{:S(2)}) collective-permute-start(bf16[64,1024]{1,0:T(8,128)(2,1)} %refs_2_.3), channel_id=1, source_target_pairs={{0,2},{1,3},{2,0},{3,1},{4,6},{5,7},{6,4},{7,5},{8,10},{9,11},{10,... | collective-permute-start | bytes 393224 | tf_op jit(solution)/shard_map/ppermute | solution.py:203
  19.3 2.3 %collective-permute-start.4 = (bf16[64,1280]{1,0:T(8,128)(2,1)}, bf16[64,1280]{1,0:T(8,128)(2,1)S(1)}, u32[]{:S(2)}, u32[]{:S(2)}) collective-permute-start(bf16[64,1280]{1,0:T(8,128)(2,1)} %refs_1_.1), channel_id=1, source_target_pairs={{0,8},{1,9},{2,10},{3,11},{4,12},{5,13},{6,14},{7,15},{8,0},{9,1},... | collective-permute-start | bytes 491528 | tf_op jit(solution)/shard_map/ppermute | solution.py:203
  21.6 0.1 collective-permute-start.11
  21.7 1.7 %collective-permute-done.13.refs_4_ = bf16[64,1024]{1,0:T(8,128)(2,1)S(1)} collective-permute-done((bf16[64,1024]{1,0:T(8,128)(2,1)}, bf16[64,1024]{1,0:T(8,128)(2,1)S(1)}, u32[]{:S(2)}, u32[]{:S(2)}) %collective-permute-start.13) | collective-permute-done | bytes 131104 | tf_op jit(solution)/shard_map/ppermute | solution.py:203
  23.3 0.0 collective-permute-start.3
  23.3 11.6 %collective-permute-done.11.refs_2_ = bf16[64,1024]{1,0:T(8,128)(2,1)S(1)} collective-permute-done((bf16[64,1024]{1,0:T(8,128)(2,1)}, bf16[64,1024]{1,0:T(8,128)(2,1)S(1)}, u32[]{:S(2)}, u32[]{:S(2)}) %collective-permute-start.11) | collective-permute-done | bytes 131104 | tf_op jit(solution)/shard_map/ppermute | solution.py:203
  34.9 0.2 collective-permute-start.6
  35.2 0.0 collective-permute-done.4.refs_6_
  35.2 0.4 collective-permute-start.5
  35.6 1.0 collective-permute-start.12
  36.6 3.8 %collective-permute-done.6.refs_8_ = bf16[64,1280]{1,0:T(8,128)(2,1)S(1)} collective-permute-done((bf16[64,1280]{1,0:T(8,128)(2,1)}, bf16[64,1280]{1,0:T(8,128)(2,1)S(1)}, u32[]{:S(2)}, u32[]{:S(2)}) %collective-permute-start.6) | collective-permute-done | bytes 163872 | tf_op jit(solution)/shard_map/ppermute | solution.py:203
  40.4 0.2 collective-permute-start.7
  40.7 2.3 %collective-permute-done.12.refs_3_ = bf16[64,1024]{1,0:T(8,128)(2,1)S(1)} collective-permute-done((bf16[64,1024]{1,0:T(8,128)(2,1)S(1)}, bf16[64,1024]{1,0:T(8,128)(2,1)S(1)}, u32[]{:S(2)}, u32[]{:S(2)}) %collective-permute-start.12) | collective-permute-done | bytes 131104 | tf_op jit(solution)/shard_map/ppermute | solution.py:203
  43.0 1.2 %collective-permute-start.8 = (bf16[64,1280]{1,0:T(8,128)(2,1)S(1)}, bf16[64,1280]{1,0:T(8,128)(2,1)S(1)}, u32[]{:S(2)}, u32[]{:S(2)}) collective-permute-start(bf16[64,1280]{1,0:T(8,128)(2,1)S(1)} %collective-permute-done.4.refs_6_), channel_id=1, source_target_pairs={{0,2},{1,3},{2,0},{3,1},{4,6},{5,7},{6,4},{7,5},{8,10},{9,11},{10,... | collective-permute-start | bytes 491528 | tf_op jit(solution)/shard_map/ppermute | solution.py:203
  44.2 0.2 collective-permute-start.9
  44.5 0.1 collective-permute-done.7.refs_9_
  44.6 0.7 copy-done.3
  45.3 3.8 %collective-permute-done.8.refs_10_ = bf16[64,1280]{1,0:T(8,128)(2,1)S(1)} collective-permute-done((bf16[64,1280]{1,0:T(8,128)(2,1)S(1)}, bf16[64,1280]{1,0:T(8,128)(2,1)S(1)}, u32[]{:S(2)}, u32[]{:S(2)}) %collective-permute-start.8) | collective-permute-done | bytes 163872 | tf_op jit(solution)/shard_map/ppermute | solution.py:203
  49.1 0.7 copy-done.5
  49.8 2.8 %collective-permute-done.9.refs_11_ = bf16[64,1280]{1,0:T(8,128)(2,1)S(1)} collective-permute-done((bf16[64,1280]{1,0:T(8,128)(2,1)S(1)}, bf16[64,1280]{1,0:T(8,128)(2,1)S(1)}, u32[]{:S(2)}, u32[]{:S(2)}) %collective-permute-start.9) | collective-permute-done | bytes 163872 | tf_op jit(solution)/shard_map/ppermute | solution.py:203
  52.6 0.7 copy-done.7
  53.3 1.1 copy-done.2
  54.4 0.9 copy-done.9
  55.3 0.9 copy-done.10
  56.2 0.1 shard_map.68
  56.3 0.0 copy-start.4
  56.3 0.9 copy-done.4
  57.2 0.9 copy-done.6
  58.1 0.9 copy-done.8
  59.0 2.0 %shard_map.69.kern_ref = bf16[1024,512]{1,0:T(8,128)(2,1)S(1)} custom-call(s32[1]{0:T(128)} %bitcast.land_ref, bf16[256,1280]{1,0:T(8,128)(2,1)S(1)} %get-tuple-element.17.refs_0_, bf16[256,1280]{1,0:T(8,128)(2,1)S(1)} %collective-permute-done.refs_1_, bf16[256,1280]{1,0:T(8,128)(2,1)S(1)} %collective-permute-done.1.refs_2_, ...), custom_call_target="tpu_custom_call" | custom-call | flops 1342177280 | bytes 4980736 | tf_op jit(solution)/shard_map/pallas_call | solution.py:42
  61.1 0.0 copy-start.11
  61.1 0.7 shard_map.70
  61.8 4.2 %collective-permute-start.17 = (bf16[512,512]{1,0:T(8,128)(2,1)S(1)}, bf16[512,512]{1,0:T(8,128)(2,1)S(1)}, u32[]{:S(2)}, u32[]{:S(2)}) collective-permute-start(bf16[512,512]{1,0:T(8,128)(2,1)S(1)} %get-tuple-element.21), channel_id=1, source_target_pairs={{0,1},{1,0},{2,3},{3,2},{4,5},{5,4},{6,7},{7,6},{8,9},{9,8},{10,11... | collective-permute-start | bytes 1572872 | tf_op jit(solution)/shard_map/ppermute | solution.py:203
  66.0 0.7 shard_map.73
  66.7 0.1 collective-permute-start.20
  66.8 0.2 convert_reduce_fusion
  67.1 0.4 collective-permute-done.17.refs_1_
  67.5 0.1 shard_map.71
  67.6 1.1 collective-permute-start.18
  68.8 0.4 select_reduce_fusion
  69.1 0.7 all_to_all.9
  69.8 5.7 %all-to-all-start = ((s32[32,1,32]{2,1,0:T(1,128)}), s32[32,1,32]{2,1,0:T(1,128)S(1)}, u32[]{:S(2)}, u32[]{:S(2)}) async-start(s32[32,1,32]{2,1,0:T(1,128)} %all_to_all.9), calls=%async_computation | async-start | bytes 32768 | tf_op jit(solution)/shard_map/all_to_all | solution.py:283
  75.6 0.1 shard_map.74
  75.7 1.2 %collective-permute-start.21 = (bf16[512,256]{1,0:T(8,128)(2,1)S(1)}, bf16[512,256]{1,0:T(8,128)(2,1)S(1)}, u32[]{:S(2)}, u32[]{:S(2)}) collective-permute-start(bf16[512,256]{1,0:T(8,128)(2,1)S(1)} %get-tuple-element.28), channel_id=1, source_target_pairs={{0,16},{16,0},{1,17},{17,1},{2,18},{18,2},{3,19},{19,3},{4,20},{20... | collective-permute-start | bytes 786440 | tf_op jit(solution)/shard_map/ppermute | solution.py:206
  76.9 0.4 fusion.refs_2_.refs_3_
  77.3 0.5 shard_map.72
  77.8 5.6 %collective-permute-done.21.refs_1_ = bf16[512,256]{1,0:T(8,128)(2,1)S(1)} collective-permute-done((bf16[512,256]{1,0:T(8,128)(2,1)S(1)}, bf16[512,256]{1,0:T(8,128)(2,1)S(1)}, u32[]{:S(2)}, u32[]{:S(2)}) %collective-permute-start.21) | collective-permute-done | bytes 262176 | tf_op jit(solution)/shard_map/ppermute | solution.py:206
  83.4 1.4 %shard_map.75 = (bf16[512,256]{1,0:T(8,128)(2,1)S(1)}, bf16[1024,512]{1,0:T(8,128)(2,1)}) custom-call(s32[1]{0:T(128)} %bitcast.land_ref, bf16[512,256]{1,0:T(8,128)(2,1)S(1)} %get-tuple-element.27.refs_0_, bf16[512,256]{1,0:T(8,128)(2,1)S(1)} %collective-permute-done.21.refs_1_, bf16[1024,256]{1,0:T(8,128)(2,1)S(1)} %get-tuple-element.29.refs_2_, ...), custom_call_target="tpu_custom_call" | custom-call | flops 268435456 | bytes 3407872 | tf_op jit(solution)/shard_map/pallas_call | solution.py:42
  84.8 6.5 %all-to-all-start.1 = ((bf16[32,32,512]{2,1,0:T(8,128)(2,1)}), bf16[32,32,512]{2,1,0:T(8,128)(2,1)S(1)}, u32[]{:S(2)}, u32[]{:S(2)}) async-start(bf16[32,32,512]{2,1,0:T(8,128)(2,1)} %bitcast.1), calls=%async_computation.1 | async-start | bytes 2097152 | tf_op jit(solution)/shard_map/all_to_all | solution.py:299
  91.3 1.2 %collective-permute-start.22 = (bf16[512,256]{1,0:T(8,128)(2,1)S(1)}, bf16[512,256]{1,0:T(8,128)(2,1)S(1)}, u32[]{:S(2)}, u32[]{:S(2)}) collective-permute-start(bf16[512,256]{1,0:T(8,128)(2,1)S(1)} %get-tuple-element.30.refs_1_), channel_id=1, source_target_pairs={{0,16},{16,0},{1,17},{17,1},{2,18},{18,2},{3,19},{19,3},{4,20},{20... | collective-permute-start | bytes 786440 | tf_op jit(solution)/shard_map/ppermute | solution.py:206
  92.6 0.3 collective-permute-start.19
  92.9 0.5 broadcast.31
  93.4 0.7 reduce.3
  94.1 0.1 reshape.26.ids_ref
  94.2 2.2 %copy-done = bf16[2048,1024]{1,0:T(8,128)(2,1)S(1)} copy-done((bf16[2048,1024]{1,0:T(8,128)(2,1)S(1)}, bf16[2048,1024]{1,0:T(8,128)(2,1)}, u32[]{:S(2)}) %copy-start) | copy-done | bytes 4194328
  96.4 3.9 %shard_map.76.refs_3_ = f32[512,2048]{1,0:T(8,128)S(1)} custom-call(s32[1]{0:T(128)} %bitcast.land_ref, bf16[512,256]{1,0:T(8,128)(2,1)S(1)} %get-tuple-element.24.refs_0_, bf16[512,256]{1,0:T(8,128)(2,1)S(1)} %get-tuple-element.30.refs_1_, bf16[2048,1024]{1,0:T(8,128)(2,1)S(1)} %copy-done), custom_call_target="tpu_custom_call" | custom-call | flops 1073741824 | bytes 8388608 | tf_op jit(solution)/shard_map/pallas_call | solution.py:314
  100.2 5.9 %collective-permute-done.22.refs_1_ = bf16[512,256]{1,0:T(8,128)(2,1)S(1)} collective-permute-done((bf16[512,256]{1,0:T(8,128)(2,1)S(1)}, bf16[512,256]{1,0:T(8,128)(2,1)S(1)}, u32[]{:S(2)}, u32[]{:S(2)}) %collective-permute-start.22) | collective-permute-done | bytes 262176 | tf_op jit(solution)/shard_map/ppermute | solution.py:206
  106.1 9.3 %collective-permute-done.19.refs_0_ = bf16[512,256]{1,0:T(8,128)(2,1)S(1)} collective-permute-done((bf16[512,256]{1,0:T(8,128)(2,1)S(1)}, bf16[512,256]{1,0:T(8,128)(2,1)S(1)}, u32[]{:S(2)}, u32[]{:S(2)}) %collective-permute-start.19) | collective-permute-done | bytes 262176 | tf_op jit(solution)/shard_map/ppermute | solution.py:206
  115.4 5.4 %shard_map.77 = f32[512,2048]{1,0:T(8,128)} custom-call(s32[1]{0:T(128)} %bitcast.land_ref, bf16[512,256]{1,0:T(8,128)(2,1)S(1)} %collective-permute-done.19.refs_0_, bf16[512,256]{1,0:T(8,128)(2,1)S(1)} %collective-permute-done.22.refs_1_, bf16[2048,1024]{1,0:T(8,128)(2,1)S(1)} %copy-done.1, f32[512,2048]{1,0:T(8,128)S(1)} %shard_map.76.refs_3_), custom_call_target="tpu_custom_call" | custom-call | flops 1073741824 | bytes 12582912 | tf_op jit(solution)/shard_map/pallas_call | solution.py:314
  120.8 1.1 shard_map.78
  (30 shorter events, 0.1 us)
Async XLA Ops:
  0.6 15.9 %collective-permute-start = (bf16[256,1280]{1,0:T(8,128)(2,1)}, bf16[256,1280]{1,0:T(8,128)(2,1)S(1)}, u32[]{:S(2)}, u32[]{:S(2)}) collective-permute-start(bf16[256,1280]{1,0:T(8,128)(2,1)} %refs_0_.1), channel_id=1, source_target_pairs={{0,16},{16,0},{1,17},{17,1},{2,18},{18,2},{3,19},{19,3},{4,20},{20... | collective-permute-start | bytes 1966088 | tf_op jit(solution)/shard_map/ppermute | solution.py:206
  1.9 51.4 %collective-permute-start.1 = (bf16[256,1280]{1,0:T(8,128)(2,1)}, bf16[256,1280]{1,0:T(8,128)(2,1)S(1)}, u32[]{:S(2)}, u32[]{:S(2)}) collective-permute-start(bf16[256,1280]{1,0:T(8,128)(2,1)} %refs_0_.1), channel_id=1, source_target_pairs={{0,1},{1,0},{2,3},{3,2},{4,5},{5,4},{6,7},{7,6},{8,9},{9,8},{10,11... | collective-permute-start | bytes 1966088 | tf_op jit(solution)/shard_map/ppermute | solution.py:203
  16.5 39.8 %collective-permute-start.2 = (bf16[256,1280]{1,0:T(8,128)(2,1)S(1)}, bf16[256,1280]{1,0:T(8,128)(2,1)S(1)}, u32[]{:S(2)}, u32[]{:S(2)}) collective-permute-start(bf16[256,1280]{1,0:T(8,128)(2,1)S(1)} %collective-permute-done.refs_1_), channel_id=1, source_target_pairs={{0,1},{1,0},{2,3},{3,2},{4,5},{5,4},{6,7},{7,6},{8,9},{9,8},{10,11... | collective-permute-start | bytes 1966088 | tf_op jit(solution)/shard_map/ppermute | solution.py:203
  18.1 5.3 %collective-permute-start.13 = (bf16[64,1024]{1,0:T(8,128)(2,1)}, bf16[64,1024]{1,0:T(8,128)(2,1)S(1)}, u32[]{:S(2)}, u32[]{:S(2)}) collective-permute-start(bf16[64,1024]{1,0:T(8,128)(2,1)} %refs_2_.3), channel_id=1, source_target_pairs={{0,2},{1,3},{2,0},{3,1},{4,6},{5,7},{6,4},{7,5},{8,10},{9,11},{10,... | collective-permute-start | bytes 393224 | tf_op jit(solution)/shard_map/ppermute | solution.py:203
  19.3 15.9 %collective-permute-start.4 = (bf16[64,1280]{1,0:T(8,128)(2,1)}, bf16[64,1280]{1,0:T(8,128)(2,1)S(1)}, u32[]{:S(2)}, u32[]{:S(2)}) collective-permute-start(bf16[64,1280]{1,0:T(8,128)(2,1)} %refs_1_.1), channel_id=1, source_target_pairs={{0,8},{1,9},{2,10},{3,11},{4,12},{5,13},{6,14},{7,15},{8,0},{9,1},... | collective-permute-start | bytes 491528 | tf_op jit(solution)/shard_map/ppermute | solution.py:203
  21.6 13.3 %collective-permute-start.11 = (bf16[64,1024]{1,0:T(8,128)(2,1)}, bf16[64,1024]{1,0:T(8,128)(2,1)S(1)}, u32[]{:S(2)}, u32[]{:S(2)}) collective-permute-start(bf16[64,1024]{1,0:T(8,128)(2,1)} %refs_2_.3), channel_id=1, source_target_pairs={{0,8},{1,9},{2,10},{3,11},{4,12},{5,13},{6,14},{7,15},{8,0},{9,1},... | collective-permute-start | bytes 393224 | tf_op jit(solution)/shard_map/ppermute | solution.py:203
  23.3 12.3 %collective-permute-start.3 = (bf16[64,1280]{1,0:T(8,128)(2,1)}, bf16[64,1280]{1,0:T(8,128)(2,1)S(1)}, u32[]{:S(2)}, u32[]{:S(2)}) collective-permute-start(bf16[64,1280]{1,0:T(8,128)(2,1)} %refs_1_.1), channel_id=1, source_target_pairs={{0,4},{1,5},{2,6},{3,7},{4,0},{5,1},{6,2},{7,3},{8,12},{9,13},{10,... | collective-permute-start | bytes 491528 | tf_op jit(solution)/shard_map/ppermute | solution.py:203
  34.9 5.5 %collective-permute-start.6 = (bf16[64,1280]{1,0:T(8,128)(2,1)}, bf16[64,1280]{1,0:T(8,128)(2,1)S(1)}, u32[]{:S(2)}, u32[]{:S(2)}) collective-permute-start(bf16[64,1280]{1,0:T(8,128)(2,1)} %refs_1_.1), channel_id=1, source_target_pairs={{0,2},{1,3},{2,0},{3,1},{4,6},{5,7},{6,4},{7,5},{8,10},{9,11},{10,... | collective-permute-start | bytes 491528 | tf_op jit(solution)/shard_map/ppermute | solution.py:203
  35.2 9.1 %collective-permute-start.5 = (bf16[64,1280]{1,0:T(8,128)(2,1)S(1)}, bf16[64,1280]{1,0:T(8,128)(2,1)S(1)}, u32[]{:S(2)}, u32[]{:S(2)}) collective-permute-start(bf16[64,1280]{1,0:T(8,128)(2,1)S(1)} %collective-permute-done.4.refs_6_), channel_id=1, source_target_pairs={{0,4},{1,5},{2,6},{3,7},{4,0},{5,1},{6,2},{7,3},{8,12},{9,13},{10,... | collective-permute-start | bytes 491528 | tf_op jit(solution)/shard_map/ppermute | solution.py:203
  35.6 7.4 %collective-permute-start.12 = (bf16[64,1024]{1,0:T(8,128)(2,1)S(1)}, bf16[64,1024]{1,0:T(8,128)(2,1)S(1)}, u32[]{:S(2)}, u32[]{:S(2)}) collective-permute-start(bf16[64,1024]{1,0:T(8,128)(2,1)S(1)} %collective-permute-done.11.refs_2_), channel_id=1, source_target_pairs={{0,4},{1,5},{2,6},{3,7},{4,0},{5,1},{6,2},{7,3},{8,12},{9,13},{10,... | collective-permute-start | bytes 393224 | tf_op jit(solution)/shard_map/ppermute | solution.py:203
  40.4 4.2 %collective-permute-start.7 = (bf16[64,1280]{1,0:T(8,128)(2,1)S(1)}, bf16[64,1280]{1,0:T(8,128)(2,1)S(1)}, u32[]{:S(2)}, u32[]{:S(2)}) collective-permute-start(bf16[64,1280]{1,0:T(8,128)(2,1)S(1)} %collective-permute-done.3.refs_5_), channel_id=1, source_target_pairs={{0,2},{1,3},{2,0},{3,1},{4,6},{5,7},{6,4},{7,5},{8,10},{9,11},{10,... | collective-permute-start | bytes 491528 | tf_op jit(solution)/shard_map/ppermute | solution.py:203
  43.0 6.1 %collective-permute-start.8 = (bf16[64,1280]{1,0:T(8,128)(2,1)S(1)}, bf16[64,1280]{1,0:T(8,128)(2,1)S(1)}, u32[]{:S(2)}, u32[]{:S(2)}) collective-permute-start(bf16[64,1280]{1,0:T(8,128)(2,1)S(1)} %collective-permute-done.4.refs_6_), channel_id=1, source_target_pairs={{0,2},{1,3},{2,0},{3,1},{4,6},{5,7},{6,4},{7,5},{8,10},{9,11},{10,... | collective-permute-start | bytes 491528 | tf_op jit(solution)/shard_map/ppermute | solution.py:203
  44.2 8.4 %collective-permute-start.9 = (bf16[64,1280]{1,0:T(8,128)(2,1)S(1)}, bf16[64,1280]{1,0:T(8,128)(2,1)S(1)}, u32[]{:S(2)}, u32[]{:S(2)}) collective-permute-start(bf16[64,1280]{1,0:T(8,128)(2,1)S(1)} %collective-permute-done.5.refs_7_), channel_id=1, source_target_pairs={{0,2},{1,3},{2,0},{3,1},{4,6},{5,7},{6,4},{7,5},{8,10},{9,11},{10,... | collective-permute-start | bytes 491528 | tf_op jit(solution)/shard_map/ppermute | solution.py:203
  44.6 0.7 copy-start.3
  45.3 15.8 %collective-permute-start.10 = (bf16[64,1024]{1,0:T(8,128)(2,1)}, bf16[64,1024]{1,0:T(8,128)(2,1)S(1)}, u32[]{:S(2)}, u32[]{:S(2)}) collective-permute-start(bf16[64,1024]{1,0:T(8,128)(2,1)} %refs_2_.3), channel_id=1, source_target_pairs={{0,4},{1,5},{2,6},{3,7},{4,0},{5,1},{6,2},{7,3},{8,12},{9,13},{10,... | collective-permute-start | bytes 393224 | tf_op jit(solution)/shard_map/ppermute | solution.py:203
  49.1 0.7 copy-start.5
  49.8 11.3 %collective-permute-start.15 = (bf16[64,1024]{1,0:T(8,128)(2,1)S(1)}, bf16[64,1024]{1,0:T(8,128)(2,1)S(1)}, u32[]{:S(2)}, u32[]{:S(2)}) collective-permute-start(bf16[64,1024]{1,0:T(8,128)(2,1)S(1)} %collective-permute-done.11.refs_2_), channel_id=1, source_target_pairs={{0,2},{1,3},{2,0},{3,1},{4,6},{5,7},{6,4},{7,5},{8,10},{9,11},{10,... | collective-permute-start | bytes 393224 | tf_op jit(solution)/shard_map/ppermute | solution.py:203
  52.6 0.7 copy-start.7
  53.3 7.8 %collective-permute-start.14 = (bf16[64,1024]{1,0:T(8,128)(2,1)S(1)}, bf16[64,1024]{1,0:T(8,128)(2,1)S(1)}, u32[]{:S(2)}, u32[]{:S(2)}) collective-permute-start(bf16[64,1024]{1,0:T(8,128)(2,1)S(1)} %collective-permute-done.13.refs_4_), channel_id=1, source_target_pairs={{0,4},{1,5},{2,6},{3,7},{4,0},{5,1},{6,2},{7,3},{8,12},{9,13},{10,... | collective-permute-start | bytes 393224 | tf_op jit(solution)/shard_map/ppermute | solution.py:203
  53.3 7.8 %collective-permute-start.16 = (bf16[64,1024]{1,0:T(8,128)(2,1)S(1)}, bf16[64,1024]{1,0:T(8,128)(2,1)S(1)}, u32[]{:S(2)}, u32[]{:S(2)}) collective-permute-start(bf16[64,1024]{1,0:T(8,128)(2,1)S(1)} %collective-permute-done.12.refs_3_), channel_id=1, source_target_pairs={{0,2},{1,3},{2,0},{3,1},{4,6},{5,7},{6,4},{7,5},{8,10},{9,11},{10,... | collective-permute-start | bytes 393224 | tf_op jit(solution)/shard_map/ppermute | solution.py:203
  53.3 1.1 copy-start.2
  54.4 0.9 copy-start.9
  55.3 0.9 copy-start.10
  56.3 0.9 copy-start.4
  57.2 0.9 copy-start.6
  58.1 0.9 copy-start.8
  61.1 4.9 %copy-start.11 = (s32[512]{0:T(512)S(1)}, s32[512]{0:T(512)}, u32[]{:S(2)}) copy-start(s32[512]{0:T(512)} %param.9) | copy-start | bytes 6148
  61.8 5.7 %collective-permute-start.17 = (bf16[512,512]{1,0:T(8,128)(2,1)S(1)}, bf16[512,512]{1,0:T(8,128)(2,1)S(1)}, u32[]{:S(2)}, u32[]{:S(2)}) collective-permute-start(bf16[512,512]{1,0:T(8,128)(2,1)S(1)} %get-tuple-element.21), channel_id=1, source_target_pairs={{0,1},{1,0},{2,3},{3,2},{4,5},{5,4},{6,7},{7,6},{8,9},{9,8},{10,11... | collective-permute-start | bytes 1572872 | tf_op jit(solution)/shard_map/ppermute | solution.py:203
  66.7 8.8 %collective-permute-start.20 = (bf16[512,512]{1,0:T(8,128)(2,1)S(1)}, bf16[512,512]{1,0:T(8,128)(2,1)S(1)}, u32[]{:S(2)}, u32[]{:S(2)}) collective-permute-start(bf16[512,512]{1,0:T(8,128)(2,1)S(1)} %get-tuple-element.26), channel_id=1, source_target_pairs={{0,1},{1,0},{2,3},{3,2},{4,5},{5,4},{6,7},{7,6},{8,9},{9,8},{10,11... | collective-permute-start | bytes 1572872 | tf_op jit(solution)/shard_map/ppermute | solution.py:203
  67.6 9.7 %collective-permute-start.18 = (bf16[512,256]{1,0:T(8,128)(2,1)S(1)}, bf16[512,256]{1,0:T(8,128)(2,1)S(1)}, u32[]{:S(2)}, u32[]{:S(2)}) collective-permute-start(bf16[512,256]{1,0:T(8,128)(2,1)S(1)} %get-tuple-element.23), channel_id=1, source_target_pairs={{0,16},{16,0},{1,17},{17,1},{2,18},{18,2},{3,19},{19,3},{4,20},{20... | collective-permute-start | bytes 786440 | tf_op jit(solution)/shard_map/ppermute | solution.py:206
  69.8 15.0 %all-to-all-start = ((s32[32,1,32]{2,1,0:T(1,128)}), s32[32,1,32]{2,1,0:T(1,128)S(1)}, u32[]{:S(2)}, u32[]{:S(2)}) async-start(s32[32,1,32]{2,1,0:T(1,128)} %all_to_all.9), calls=%async_computation | async-start | bytes 32768 | tf_op jit(solution)/shard_map/all_to_all | solution.py:283
  75.7 7.7 %collective-permute-start.21 = (bf16[512,256]{1,0:T(8,128)(2,1)S(1)}, bf16[512,256]{1,0:T(8,128)(2,1)S(1)}, u32[]{:S(2)}, u32[]{:S(2)}) collective-permute-start(bf16[512,256]{1,0:T(8,128)(2,1)S(1)} %get-tuple-element.28), channel_id=1, source_target_pairs={{0,16},{16,0},{1,17},{17,1},{2,18},{18,2},{3,19},{19,3},{4,20},{20... | collective-permute-start | bytes 786440 | tf_op jit(solution)/shard_map/ppermute | solution.py:206
  84.8 36.0 %all-to-all-start.1 = ((bf16[32,32,512]{2,1,0:T(8,128)(2,1)}), bf16[32,32,512]{2,1,0:T(8,128)(2,1)S(1)}, u32[]{:S(2)}, u32[]{:S(2)}) async-start(bf16[32,32,512]{2,1,0:T(8,128)(2,1)} %bitcast.1), calls=%async_computation.1 | async-start | bytes 2097152 | tf_op jit(solution)/shard_map/all_to_all | solution.py:299
  91.3 14.8 %collective-permute-start.22 = (bf16[512,256]{1,0:T(8,128)(2,1)S(1)}, bf16[512,256]{1,0:T(8,128)(2,1)S(1)}, u32[]{:S(2)}, u32[]{:S(2)}) collective-permute-start(bf16[512,256]{1,0:T(8,128)(2,1)S(1)} %get-tuple-element.30.refs_1_), channel_id=1, source_target_pairs={{0,16},{16,0},{1,17},{17,1},{2,18},{18,2},{3,19},{19,3},{4,20},{20... | collective-permute-start | bytes 786440 | tf_op jit(solution)/shard_map/ppermute | solution.py:206
  92.6 22.8 %collective-permute-start.19 = (bf16[512,256]{1,0:T(8,128)(2,1)S(1)}, bf16[512,256]{1,0:T(8,128)(2,1)S(1)}, u32[]{:S(2)}, u32[]{:S(2)}) collective-permute-start(bf16[512,256]{1,0:T(8,128)(2,1)S(1)} %get-tuple-element.24.refs_0_), channel_id=1, source_target_pairs={{0,16},{16,0},{1,17},{17,1},{2,18},{18,2},{3,19},{19,3},{4,20},{20... | collective-permute-start | bytes 786440 | tf_op jit(solution)/shard_map/ppermute | solution.py:206
  94.2 2.2 %copy-start = (bf16[2048,1024]{1,0:T(8,128)(2,1)S(1)}, bf16[2048,1024]{1,0:T(8,128)(2,1)}, u32[]{:S(2)}) copy-start(bf16[2048,1024]{1,0:T(8,128)(2,1)} %refs_2_.5) | copy-start | bytes 12582916
  96.4 19.1 %copy-start.1 = (bf16[2048,1024]{1,0:T(8,128)(2,1)S(1)}, bf16[2048,1024]{1,0:T(8,128)(2,1)}, u32[]{:S(2)}) copy-start(bf16[2048,1024]{1,0:T(8,128)(2,1)} %refs_2_.5) | copy-start | bytes 12582916

commit v2 on v1

--- a/solution.py
+++ b/solution.py
@@ -10,7 +10,7 @@
 
 EPSILON = 1e-06
 SHARPNESS = 6.0
-FACTOR_PARTS = 2
+LANES = 128
 VMEM = pl.BlockSpec(memory_space=pltpu.VMEM)
 SMEM = pl.BlockSpec(memory_space=pltpu.SMEM)
 
@@ -23,6 +23,10 @@
 
 def partner(index, size, step):
     return index ^ step if size & (size - 1) == 0 else (index + step) % size
+
+
+def offset_of(target, own, size):
+    return target ^ own if size & (size - 1) == 0 else (target - own + size) % size
 
 
 def axis_perm(sizes, axis, step):
@@ -82,7 +86,7 @@
             out_ref[pl.ds(offset, rows), :] = jnp.exp(SHARPNESS * (similarity - 1.0)).astype(out_ref.dtype)
 
 
-def partial_body(land_count, cores, pieces, part, land_ref, kern_ref, *refs):
+def partial_body(land_count, cores, pieces, start, land_ref, kern_ref, *refs):
     piece_refs, (own_ref, *others, block) = refs[:pieces], refs[pieces:]
     depth, full = piece_refs[0].shape
     keep_width = full // land_count
@@ -90,7 +94,7 @@
     rows = own_ref.shape[0]
     for s in range(land_count):
         source = lax.rem(land_ref[0] + s, land_count)
-        columns = pl.ds(pl.multiple_of(source * keep_width + part * width, 128), width)
+        columns = pl.ds(pl.multiple_of(source * keep_width + start, LANES), width)
         for i, piece in enumerate(piece_refs):
             block[i * depth : (i + 1) * depth] = piece[:, columns]
         for g in reversed(range(cores)):
@@ -109,19 +113,69 @@
         out[...] = total.astype(out.dtype)
 
 
-def pick_body(count, land_ref, *refs):
-    *ins, pick_ref, feat_ref, out_ref = refs
+def pick_body(count, tags, land_ref, *refs):
+    ins, (pick_ref, *refs) = refs[:count], refs[count:]
+    feat_ref, *outs = refs[tags:]
     total = ins[0][...].astype(jnp.float32)
-    for part in ins[1:count]:
+    for part in ins[1:]:
         total = total + part[...].astype(jnp.float32)
     features = total.astype(feat_ref.dtype)
     feat_ref[...] = features
-    start = 0
-    for done in ins[count:]:
-        start = done.shape[1]
-        out_ref[:, :start] = done[...]
-    value = jnp.dot(pick_ref[...], features, preferred_element_type=jnp.float32)
-    out_ref[:, start:] = value.astype(out_ref.dtype)
+    width, rows = features.shape[1], outs[0].shape[0]
+    for i, out in enumerate(outs):
+        pick = pick_ref[i * rows : (i + 1) * rows]
+        out[:, :width] = jnp.dot(pick, features, preferred_element_type=jnp.float32).astype(out.dtype)
+        if tags:
+            value = jnp.dot(pick, refs[0][...], preferred_element_type=jnp.float32)
+            out[:, width:] = value.astype(out.dtype)
+
+
+def take_body(plan, land_ref, *refs):
+    *ins, out_ref = refs
+    at = 0
+    for i, start, rows in plan:
+        out_ref[at : at + rows] = ins[i][start : start + rows]
+        at += rows
+
+
+def over_slots(match, values):
+    return lax.dot_general(match, values, (((0,), (0,)), ((), ())), preferred_element_type=jnp.float32)
+
+
+def peer_mean_body(plan, peers, slot_count, table_ref, *refs):
+    ins, refs = refs[: 1 + max(i for i, _, _ in plan)], refs[1 + max(i for i, _, _ in plan) :]
+    own_ref, *sends, match_ref, count_ref, arrived, matched = refs
+    take_body(plan, table_ref, *ins, arrived)
+    slots, own_width = matched.shape
+    values = arrived[:, : own_ref.shape[1]]
+    tags = arrived[:, own_ref.shape[1] :].astype(jnp.float32)
+    lane = lax.broadcasted_iota(jnp.int32, (slots, own_width), 1).astype(jnp.float32)
+    ones = jnp.ones((slots, own_width), jnp.bfloat16)
+    for s, out in enumerate([own_ref, *sends]):
+        match = (tags == lane + (1 + s * own_width)).astype(jnp.float32).astype(jnp.bfloat16)
+        counts = over_slots(match, ones)
+        out[...] = (over_slots(match, values) / jnp.maximum(counts, 1.0)).astype(out.dtype)
+        if s == 0:
+            matched[...] = match
+            count_ref[...] = counts
+    for d in range(peers):
+        start = pl.multiple_of(table_ref[d], slot_count)
+        match_ref[d * slot_count : (d + 1) * slot_count] = matched[pl.ds(start, slot_count), :]
+
+
+def join_body(land_count, land_ref, match_ref, count_ref, arrived_ref, *refs):
+    *means, out_ref = refs
+    slots, width = match_ref.shape[0], arrived_ref.shape[1]
+    first = means[0].shape[1]
+    keep_width = first + width
+    scale = jnp.maximum(count_ref[:, 0:1], 1.0)
+    for j in range(land_count):
+        sums = over_slots(match_ref[...], arrived_ref[j * slots : (j + 1) * slots])
+        out_ref[:, j * keep_width + first : (j + 1) * keep_width] = sums / scale
+    for s, mean in enumerate(means):
+        source = lax.rem(land_ref[0] + land_count - s, land_count)
+        columns = pl.ds(pl.multiple_of(source * keep_width, LANES), first)
+        out_ref[:, columns] = mean[...].astype(jnp.float32)
 
 
 def square_sum(parts):
@@ -133,11 +187,13 @@
 
 
 def cross_sum(feats, cent_ref, first, land_count, parts, land_ref):
-    width = feats[0].shape[1]
-    cross = None
+    keep_width = sum(feat.shape[1] for feat in feats[:parts])
+    cross, at = None, 0
     for i, feat in enumerate(feats):
+        at = 0 if i % parts == 0 else at
         source = lax.rem(land_ref[0] + first + i // parts, land_count)
-        columns = pl.ds(pl.multiple_of((source * parts + i % parts) * width, 128), width)
+        columns = pl.ds(pl.multiple_of(source * keep_width + at, LANES), feat.shape[1])
+        at += feat.shape[1]
         term = lax.dot_general(
             feat[...], cent_ref[:, columns], (((1,), (1,)), ((), ())), preferred_element_type=jnp.float32
         )
@@ -180,8 +236,11 @@
         out_ref[:, j * width : (j + 1) * width] = sums / jnp.maximum(counts, 1.0)
 
 
-def factor_parts(feat_width, land_count):
-    return FACTOR_PARTS if feat_width % (128 * land_count * FACTOR_PARTS) == 0 else 1
+def column_parts(feat_width, land_count, own_width):
+    keep_width = feat_width // land_count
+    if keep_width > LANES and own_width == LANES and land_count * own_width <= 256:
+        return [LANES, keep_width - LANES]
+    return [keep_width]
 
 
 def local(embeddings, landmarks, factor, centroids, assignment):
@@ -228,9 +287,9 @@
     row_pieces = [embeddings] + [land_send(embeddings, land_count - k) for k in range(1, land_count)]
     row_pieces = row_pieces + [move(p, 2, k) for k in range(1, cores) for p in row_pieces]
     marks = along_y(along_z(landmarks), False)
-    parts = factor_parts(feat_width, land_count)
-    keep_width = feat_width // land_count
-    width = keep_width // parts
+    own_width = centroids.shape[0] // dp_count
+    widths = column_parts(feat_width, land_count, own_width)
+    parts = len(widths)
     factors = along_y(along_z(factor), sizes[0] > 1)
 
     rows_all = group_rows * cores
@@ -250,9 +309,9 @@
         flops=2 * rows_all * depth_all * embed_width,
     )
     keeps, sends = [], []
-    for h in range(parts):
+    for h, width in enumerate(widths):
         own, *others = call(
-            functools.partial(partial_body, land_count, cores, len(marks), h),
+            functools.partial(partial_body, land_count, cores, len(factors), sum(widths[:h])),
             [shape(group_rows, land_count * width, f32)]
             + [shape(group_rows, land_count * width, bf16)] * (cores - 1),
             [kern] + factors,
@@ -267,43 +326,97 @@
         keeps.append(keep)
         sends.append([land_send(x, s) for s, x in enumerate(send, 1)])
 
-    own_width = centroids.shape[0] // dp_count
+    assignment, dp_id, land_late, _ = lax.optimization_barrier(
+        (assignment, lax.axis_index("dp"), land_id, keeps[0])
+    )
     slot_count = 2 * max(1, group_rows // (land_count * dp_count))
-    slot_total = land_count * dp_count * slot_count
-    everyone = ("land", "dp")
+    peer_slots = land_count * slot_count
+    slot_total = dp_count * peer_slots
     slice_id = assignment // own_width
     local_id = assignment % own_width
     row_pos = lax.iota(jnp.int32, group_rows)
     earlier = (slice_id[None, :] == slice_id[:, None]) & (row_pos[None, :] < row_pos[:, None])
     slot_rank = jnp.sum(earlier.astype(jnp.int32), axis=1)
-    slot_of = slice_id * slot_count + slot_rank
-    slot_match = lax.iota(jnp.int32, slot_total)[:, None] == slot_of[None, :]
-    slot_ids = jnp.max(jnp.where(slot_match, local_id[None, :], -1), axis=1)
-    slot_pick = slot_match.astype(bf16)
-    arrived_ids = lax.all_to_all(
-        slot_ids.reshape(land_count * dp_count, slot_count), everyone, split_axis=0, concat_axis=0, tiled=True
-    )
-    arrived_ids = arrived_ids.reshape(1, slot_total)
-
-    mine, outgoing = [], None
-    for h in range(parts):
-        before = [outgoing] if h else []
-        feat, outgoing = call(
-            functools.partial(pick_body, land_count),
-            [shape(group_rows, width, bf16), shape(slot_total, (h + 1) * width, bf16)],
-            [keeps[h]] + sends[h] + before + [slot_pick],
+    slot_pos = lax.iota(jnp.int32, slot_total)[:, None]
+    owner_match = slot_pos == (slice_id * slot_count + slot_rank)[None, :]
+    everyone = ("land", "dp")
+
+    def pick(h, blocks, rows, one_hot, tags):
+        feat, *picked = call(
+            functools.partial(pick_body, land_count, len(tags)),
+            [shape(group_rows, widths[h], bf16)]
+            + [shape(rows, widths[h] + sum(t.shape[1] for t in tags), bf16)] * blocks,
+            [keeps[h]] + sends[h] + [one_hot.astype(bf16)] + tags,
             land,
-            flops=2 * group_rows * slot_total * width,
+            flops=2 * group_rows * blocks * rows * widths[h],
         )
         mine.append(feat)
+        return picked
+
+    mine, means = [], []
+    if parts > 1:
+        outer, middle, _ = sizes
+
+        def places(index):
+            return index // (middle * cores), index // cores % middle, index % cores
+
+        target_dp = slice_id % dp_count
+        land_offset = lax.rem(slice_id // dp_count - land_late + land_count, land_count)
+        here = places(dp_id)
+        away = [offset_of(t, o, n) for t, o, n in zip(places(target_dp), here, sizes)]
+        block_of = (away[0] * middle + away[1]) * cores + away[2]
+        peer_match = slot_pos == (block_of * peer_slots + land_offset * slot_count + slot_rank)[None, :]
+        tag = (land_offset * own_width + local_id + 1).astype(f32).astype(bf16)
+        tags = jnp.broadcast_to(tag[:, None], (group_rows, own_width))
+        order = lax.iota(jnp.int32, dp_count)
+        near = [offset_of(o, d, n) for o, d, n in zip(here, places(order), sizes)]
+        table = ((near[2] * middle + near[1]) * outer + near[0]) * peer_slots
+        held = pick(0, outer, middle * cores * peer_slots, peer_match, [tags])
+        held = [held[0]] + [move(held[k], 0, k) for k in range(1, outer)]
+        tagged = widths[0] + own_width
+
+        def take(plan, ins):
+            rows = sum(n for _, _, n in plan)
+            return call(functools.partial(take_body, plan), [shape(rows, tagged, bf16)], ins, land)[0]
+
+        plan = [(i, 0, cores * peer_slots) for i in range(outer)]
+        for k in range(1, middle):
+            line = [(i, k * cores * peer_slots, cores * peer_slots) for i in range(outer)]
+            held.append(move(take(line, held[:outer]), 1, k))
+            plan += [(len(held) - 1, i * cores * peer_slots, cores * peer_slots) for i in range(outer)]
+        own_plan = [(i, start, peer_slots) for i, start, _ in plan]
+        along = len(held)
+        for k in range(1, cores):
+            line = [(i, start + k * peer_slots, peer_slots) for i, start, _ in plan]
+            held.append(move(take(line, held[:along]), 2, k))
+            own_plan.append((len(held) - 1, 0, len(plan) * peer_slots))
+        mean, *results = call(
+            functools.partial(peer_mean_body, own_plan, dp_count, slot_count),
+            [shape(own_width, widths[0], f32)]
+            + [shape(own_width, widths[0], bf16)] * (land_count - 1)
+            + [shape(dp_count * slot_count, own_width, bf16), shape(own_width, own_width, f32)],
+            held,
+            table,
+            scratch=[((slot_total, tagged), bf16), ((slot_total, own_width), bf16)],
+            flops=4 * land_count * own_width * slot_total * widths[0],
+        )
+        *far, slot_owner, counts = results
+        means = [mean] + [land_send(m, s) for s, m in enumerate(far, 1)]
+    else:
+        slot_ids = jnp.max(jnp.where(owner_match, local_id[None, :], -1), axis=1)
+        arrived_ids = lax.all_to_all(
+            slot_ids.reshape(land_count * dp_count, slot_count), everyone, split_axis=0, concat_axis=0, tiled=True
+        )
+        arrived_ids = arrived_ids.reshape(1, slot_total)
+    (outgoing,) = pick(parts - 1, 1, slot_total, owner_match, [])
     arrived = lax.all_to_all(
-        outgoing.reshape(land_count * dp_count, slot_count, keep_width),
+        outgoing.reshape(land_count * dp_count, slot_count, widths[-1]),
         everyone,
         split_axis=0,
         concat_axis=0,
         tiled=True,
     )
-    arrived = arrived.reshape(slot_total, keep_width)
+    arrived = arrived.reshape(slot_total, widths[-1])
     others = [land_send(mine[h], land_count - s) for s in range(1, land_count) for h in range(parts)]
 
     cent_block = centroids.shape[0]
@@ -316,13 +429,13 @@
             grid=(cent_block // block,),
             out_shape=shape(group_rows, cent_block, f32),
             in_specs=[SMEM]
-            + [pl.BlockSpec((group_rows, width), lambda i: (0, 0))] * len(feats)
+            + [pl.BlockSpec(f.shape, lambda i: (0, 0)) for f in feats]
             + [pl.BlockSpec((block, feat_width), lambda i: (i, 0))]
             + [tile] * len(more),
             out_specs=tile,
             scratch_shapes=[pltpu.VMEM((group_rows, 1), f32)],
             cost_estimate=pl.CostEstimate(
-                flops=2 * group_rows * cent_block * width * len(feats),
+                flops=2 * group_rows * cent_block * sum(f.shape[1] for f in feats),
                 bytes_accessed=2 * cent_block * feat_width + 4 * group_rows * cent_block * (1 + len(more)),
                 transcendentals=0,
             ),
@@ -331,12 +444,12 @@
 
     near = by_block(near_body, mine, [])
     distances = by_block(distance_body, others, [near])
+    if parts > 1:
+        body, ins = functools.partial(join_body, land_count), [slot_owner, counts, arrived] + means
+    else:
+        body, ins = functools.partial(mean_body, land_count), [arrived_ids, arrived]
     (new_centroids,) = call(
-        functools.partial(mean_body, land_count),
-        [shape(own_width, feat_width, f32)],
-        [arrived_ids, arrived],
-        land,
-        flops=2 * own_width * slot_total * keep_width,
+        body, [shape(own_width, feat_width, f32)], ins, land, flops=2 * own_width * slot_total * widths[-1]
     )
     return (distances, new_centroids)
 

time: 124 us -> 142 us (1.15); the launches traced: 122 us -> 142 us
  waiting for transfers between devices: 61.1 us -> 79 us
  local copies, waits for them, and re-layouts: 11.1 us -> 3.04 us
  Pallas kernels: 16 us -> 22.3 us
  starting transfers between devices: 31.2 us -> 35.8 us
    ppermute x18 -> x23, waiting for transfers between devices: 26.7 us -> 48.8 us  [move(): return lax.ppermute(x, 'dp', axis_perm(sizes, axis, step))]
    ppermute x18 -> x23, starting transfers between devices: 13.7 us -> 21.7 us  [move(): return lax.ppermute(x, 'dp', axis_perm(sizes, axis, step))]
    unnamed x24 -> x10, local copies, waits for them, and re-layouts: 9.83 us -> 2.91 us
    pallas_call x9 -> x12, Pallas kernels: 6.73 us -> 12.4 us  [call(): pl.pallas_call(body, out_shape=list(outs), in_specs=[SMEM] + [VMEM] * len...]
    all_to_all x2 -> x1, starting transfers between devices: 12.2 us -> 6.84 us  [local(): lax.all_to_all(outgoing.reshape(land_count * dp_count, slot_count, widths...]
    ppermute x5 -> x6, waiting for transfers between devices: 34.4 us -> 30.2 us  [land_send(): lax.ppermute(x, 'land', [(s, (s + step) % land_count) for s in range(land...]
    ppermute x5 -> x6, starting transfers between devices: 5.19 us -> 7.26 us  [land_send(): lax.ppermute(x, 'land', [(s, (s + step) % land_count) for s in range(land...]
  transfers between devices with their start and end apart: 25 -> 30, of which waited for: 12 -> 15; matrix products, arithmetic and copies ran while one was open for 2% -> 1% of each run, Pallas kernels for 12% -> 11%
where the time goes in v2:
time: 142 us
  waiting for transfers between devices  79 us (56%)
  starting transfers between devices  35.8 us (25%)
  Pallas kernels  22.3 us (16%)
  local copies, waits for them, and re-layouts  3.04 us (2%)
    ppermute x23, waiting for transfers between devices, move(): return lax.ppermute(x, 'dp', axis_perm(sizes, axis, step))  48.8 us
    ppermute x6, waiting for transfers between devices, land_send(): lax.ppermute(x, 'land', [(s, (s + step) % land_count) for s in range(land...  30.2 us
    ppermute x23, starting transfers between devices, move(): return lax.ppermute(x, 'dp', axis_perm(sizes, axis, step))  21.7 us
    pallas_call x12, Pallas kernels, call(): pl.pallas_call(body, out_shape=list(outs), in_specs=[SMEM] + [VMEM] * len...  12.4 us
    pallas_call x2, Pallas kernels, by_block(): pl.pallas_call(functools.partial(body, land_count, parts), grid=(cent_blo...  9.89 us
    ppermute x6, starting transfers between devices, land_send(): lax.ppermute(x, 'land', [(s, (s + step) % land_count) for s in range(land...  7.26 us
    all_to_all x1, starting transfers between devices, local(): lax.all_to_all(outgoing.reshape(land_count * dp_count, slot_count, widths...  6.84 us
    unnamed x10, local copies, waits for them, and re-layouts  2.91 us
  transfers between devices with their start and end apart: 30, of which 15 were waited for; matrix products, arithmetic and copies ran while one was open for 1% of the time, Pallas kernels for 11%

profile of v2, /device:TPU:9, one launch (start us, length us, event | category | flops | bytes accessed | tf_op | source)
XLA Modules:
  0.0 142.2 jit_solution(13072279829968266548)
XLA Ops:
  0.6 1.3 collective-permute-start
  1.9 1.0 collective-permute-start.1
  2.9 13.7 %collective-permute-done.refs_1_ = bf16[256,1280]{1,0:T(8,128)(2,1)S(1)} collective-permute-done((bf16[256,1280]{1,0:T(8,128)(2,1)}, bf16[256,1280]{1,0:T(8,128)(2,1)S(1)}, u32[]{:S(2)}, u32[]{:S(2)}) %collective-permute-start) | collective-permute-done | bytes 655392 | tf_op jit(solution)/shard_map/ppermute | solution.py:265
  16.5 1.5 %collective-permute-start.2 = (bf16[256,1280]{1,0:T(8,128)(2,1)S(1)}, bf16[256,1280]{1,0:T(8,128)(2,1)S(1)}, u32[]{:S(2)}, u32[]{:S(2)}) collective-permute-start(bf16[256,1280]{1,0:T(8,128)(2,1)S(1)} %collective-permute-done.refs_1_), channel_id=1, source_target_pairs={{0,1},{1,0},{2,3},{3,2},{4,5},{5,4},{6,7},{7,6},{8,9},{9,8},{10,11... | collective-permute-start | bytes 1966088 | tf_op jit(solution)/shard_map/ppermute | solution.py:262
  18.1 1.2 collective-permute-start.13
  19.3 2.3 %collective-permute-start.4 = (bf16[64,1280]{1,0:T(8,128)(2,1)}, bf16[64,1280]{1,0:T(8,128)(2,1)S(1)}, u32[]{:S(2)}, u32[]{:S(2)}) collective-permute-start(bf16[64,1280]{1,0:T(8,128)(2,1)} %refs_1_.1), channel_id=1, source_target_pairs={{0,8},{1,9},{2,10},{3,11},{4,12},{5,13},{6,14},{7,15},{8,0},{9,1},... | collective-permute-start | bytes 491528 | tf_op jit(solution)/shard_map/ppermute | solution.py:262
  21.6 0.1 collective-permute-start.11
  21.7 1.7 %collective-permute-done.13.refs_4_ = bf16[64,1024]{1,0:T(8,128)(2,1)S(1)} collective-permute-done((bf16[64,1024]{1,0:T(8,128)(2,1)}, bf16[64,1024]{1,0:T(8,128)(2,1)S(1)}, u32[]{:S(2)}, u32[]{:S(2)}) %collective-permute-start.13) | collective-permute-done | bytes 131104 | tf_op jit(solution)/shard_map/ppermute | solution.py:262
  23.3 0.0 collective-permute-start.3
  23.3 11.6 %collective-permute-done.11.refs_2_ = bf16[64,1024]{1,0:T(8,128)(2,1)S(1)} collective-permute-done((bf16[64,1024]{1,0:T(8,128)(2,1)}, bf16[64,1024]{1,0:T(8,128)(2,1)S(1)}, u32[]{:S(2)}, u32[]{:S(2)}) %collective-permute-start.11) | collective-permute-done | bytes 131104 | tf_op jit(solution)/shard_map/ppermute | solution.py:262
  34.9 0.2 collective-permute-start.6
  35.2 0.0 collective-permute-done.4.refs_6_
  35.2 0.4 collective-permute-start.5
  35.6 0.0 collective-permute-done.3.refs_5_
  35.6 1.0 collective-permute-start.12
  36.6 3.8 %collective-permute-done.6.refs_8_ = bf16[64,1280]{1,0:T(8,128)(2,1)S(1)} collective-permute-done((bf16[64,1280]{1,0:T(8,128)(2,1)}, bf16[64,1280]{1,0:T(8,128)(2,1)S(1)}, u32[]{:S(2)}, u32[]{:S(2)}) %collective-permute-start.6) | collective-permute-done | bytes 163872 | tf_op jit(solution)/shard_map/ppermute | solution.py:262
  40.4 0.2 collective-permute-start.7
  40.7 2.3 %collective-permute-done.12.refs_3_ = bf16[64,1024]{1,0:T(8,128)(2,1)S(1)} collective-permute-done((bf16[64,1024]{1,0:T(8,128)(2,1)S(1)}, bf16[64,1024]{1,0:T(8,128)(2,1)S(1)}, u32[]{:S(2)}, u32[]{:S(2)}) %collective-permute-start.12) | collective-permute-done | bytes 131104 | tf_op jit(solution)/shard_map/ppermute | solution.py:262
  43.0 1.2 collective-permute-start.8
  44.2 0.2 collective-permute-start.9
  44.5 0.1 collective-permute-done.7.refs_9_
  44.6 0.0 collective-permute-start.10
  44.6 4.5 %collective-permute-done.8.refs_10_ = bf16[64,1280]{1,0:T(8,128)(2,1)S(1)} collective-permute-done((bf16[64,1280]{1,0:T(8,128)(2,1)S(1)}, bf16[64,1280]{1,0:T(8,128)(2,1)S(1)}, u32[]{:S(2)}, u32[]{:S(2)}) %collective-permute-start.8) | collective-permute-done | bytes 163872 | tf_op jit(solution)/shard_map/ppermute | solution.py:262
  49.1 3.6 %collective-permute-done.9.refs_11_ = bf16[64,1280]{1,0:T(8,128)(2,1)S(1)} collective-permute-done((bf16[64,1280]{1,0:T(8,128)(2,1)S(1)}, bf16[64,1280]{1,0:T(8,128)(2,1)S(1)}, u32[]{:S(2)}, u32[]{:S(2)}) %collective-permute-start.9) | collective-permute-done | bytes 163872 | tf_op jit(solution)/shard_map/ppermute | solution.py:262
  52.8 1.1 copy-done.1
  53.8 0.9 copy-done.2
  54.8 0.9 copy-done.3
  55.7 0.1 shard_map.68
  55.7 2.0 %shard_map.69.kern_ref = bf16[1024,512]{1,0:T(8,128)(2,1)S(1)} custom-call(s32[1]{0:T(128)} %bitcast.land_ref, bf16[256,1280]{1,0:T(8,128)(2,1)S(1)} %get-tuple-element.27.refs_0_, bf16[256,1280]{1,0:T(8,128)(2,1)S(1)} %collective-permute-done.refs_1_, bf16[256,1280]{1,0:T(8,128)(2,1)S(1)} %collective-permute-done.1.refs_2_, ...), custom_call_target="tpu_custom_call" | custom-call | flops 1342177280 | bytes 4980736 | tf_op jit(solution)/shard_map/pallas_call | solution.py:46
  57.8 3.0 %shard_map.73 = (f32[512,768]{1,0:T(8,128)S(1)}, bf16[512,768]{1,0:T(8,128)(2,1)}) custom-call(s32[1]{0:T(128)} %bitcast.land_ref, bf16[1024,512]{1,0:T(8,128)(2,1)S(1)} %shard_map.69.kern_ref, bf16[64,1024]{1,0:T(8,128)(2,1)S(1)} %get-tuple-element.29.refs_0_, bf16[64,1024]{1,0:T(8,128)(2,1)} %collective-permute-done.10.refs_1_, ...), custom_call_target="tpu_custom_call" | custom-call | flops 805306368 | bytes 4456448 | tf_op jit(solution)/shard_map/pallas_call | solution.py:46
  60.8 4.0 %collective-permute-start.20 = (bf16[512,768]{1,0:T(8,128)(2,1)}, bf16[512,768]{1,0:T(8,128)(2,1)S(1)}, u32[]{:S(2)}, u32[]{:S(2)}) collective-permute-start(bf16[512,768]{1,0:T(8,128)(2,1)} %get-tuple-element.39), channel_id=1, source_target_pairs={{0,1},{1,0},{2,3},{3,2},{4,5},{5,4},{6,7},{7,6},{8,9},{9,8},{10,11... | collective-permute-start | bytes 2359304 | tf_op jit(solution)/shard_map/ppermute | solution.py:262
  64.8 2.5 %shard_map.70 = (f32[512,256]{1,0:T(8,128)S(1)}, bf16[512,256]{1,0:T(8,128)(2,1)}) custom-call(s32[1]{0:T(128)} %bitcast.land_ref, bf16[1024,512]{1,0:T(8,128)(2,1)S(1)} %shard_map.69.kern_ref, bf16[64,1024]{1,0:T(8,128)(2,1)S(1)} %get-tuple-element.29.refs_0_, bf16[64,1024]{1,0:T(8,128)(2,1)} %collective-permute-done.10.refs_1_, ...), custom_call_target="tpu_custom_call" | custom-call | flops 268435456 | bytes 2883584 | tf_op jit(solution)/shard_map/pallas_call | solution.py:46
  67.3 0.0 collective-permute-start.17
  67.3 1.7 %collective-permute-done.17.refs_1_ = bf16[512,256]{1,0:T(8,128)(2,1)S(1)} collective-permute-done((bf16[512,256]{1,0:T(8,128)(2,1)}, bf16[512,256]{1,0:T(8,128)(2,1)S(1)}, u32[]{:S(2)}, u32[]{:S(2)}) %collective-permute-start.17) | collective-permute-done | bytes 262176 | tf_op jit(solution)/shard_map/ppermute | solution.py:262
  69.1 0.1 shard_map.71
  69.2 0.2 convert_reduce_fusion
  69.5 0.1 shard_map.74
  69.6 1.1 collective-permute-start.21
  70.8 0.4 fusion.1.refs_2_
  71.2 9.0 %collective-permute-done.21.refs_1_ = bf16[512,384]{1,0:T(8,128)(2,1)S(1)} collective-permute-done((bf16[512,384]{1,0:T(8,128)(2,1)S(1)}, bf16[512,384]{1,0:T(8,128)(2,1)S(1)}, u32[]{:S(2)}, u32[]{:S(2)}) %collective-permute-start.21) | collective-permute-done | bytes 393248 | tf_op jit(solution)/shard_map/ppermute | solution.py:265
  80.2 1.6 %shard_map.75 = (bf16[512,384]{1,0:T(8,128)(2,1)S(1)}, bf16[1024,384]{1,0:T(8,128)(2,1)}) custom-call(s32[1]{0:T(128)} %bitcast.land_ref, bf16[512,384]{1,0:T(8,128)(2,1)S(1)} %get-tuple-element.40.refs_0_, bf16[512,384]{1,0:T(8,128)(2,1)S(1)} %collective-permute-done.21.refs_1_, bf16[1024,512]{1,0:T(8,128)(2,1)S(1)} %fusion.1.refs_2_), custom_call_target="tpu_custom_call" | custom-call | flops 402653184 | bytes 3014656 | tf_op jit(solution)/shard_map/pallas_call | solution.py:46
  81.9 6.8 %all-to-all-start = ((bf16[32,32,384]{2,1,0:T(8,128)(2,1)}), bf16[32,32,384]{2,1,0:T(8,128)(2,1)S(1)}, u32[]{:S(2)}, u32[]{:S(2)}) async-start(bf16[32,32,384]{2,1,0:T(8,128)(2,1)} %bitcast.1), calls=%async_computation | async-start | bytes 1572864 | tf_op jit(solution)/shard_map/all_to_all | solution.py:412
  88.7 1.2 collective-permute-start.18
  90.0 0.4 fusion.refs_2_
  90.4 7.6 %collective-permute-done.18.refs_1_ = bf16[512,128]{1,0:T(8,128)(2,1)S(1)} collective-permute-done((bf16[512,128]{1,0:T(8,128)(2,1)S(1)}, bf16[512,128]{1,0:T(8,128)(2,1)S(1)}, u32[]{:S(2)}, u32[]{:S(2)}) %collective-permute-start.18) | collective-permute-done | bytes 131104 | tf_op jit(solution)/shard_map/ppermute | solution.py:265
  97.9 0.1 broadcast_in_dim.2.refs_3_
  98.1 0.0 copy-start
  98.1 0.7 shard_map.72
  98.8 1.5 %collective-permute-start.23 = (bf16[256,256]{1,0:T(8,128)(2,1)S(1)}, bf16[256,256]{1,0:T(8,128)(2,1)S(1)}, u32[]{:S(2)}, u32[]{:S(2)}) collective-permute-start(bf16[256,256]{1,0:T(8,128)(2,1)S(1)} %get-tuple-element.44), channel_id=1, source_target_pairs={{0,4},{1,5},{2,6},{3,7},{4,0},{5,1},{6,2},{7,3},{8,12},{9,13},{10,... | collective-permute-start | bytes 393224 | tf_op jit(solution)/shard_map/ppermute | solution.py:262
  100.3 3.4 %collective-permute-start.24 = (bf16[256,256]{1,0:T(8,128)(2,1)S(1)}, bf16[256,256]{1,0:T(8,128)(2,1)S(1)}, u32[]{:S(2)}, u32[]{:S(2)}) collective-permute-start(bf16[256,256]{1,0:T(8,128)(2,1)S(1)} %get-tuple-element.45), channel_id=1, source_target_pairs={{0,8},{1,9},{2,10},{3,11},{4,12},{5,13},{6,14},{7,15},{8,0},{9,1},... | collective-permute-start | bytes 393224 | tf_op jit(solution)/shard_map/ppermute | solution.py:262
  103.7 0.2 collective-permute-start.25
  103.9 1.1 collective-permute-done.23.refs_1_
  104.9 9.5 %collective-permute-done.24.refs_2_ = bf16[256,256]{1,0:T(8,128)(2,1)S(1)} collective-permute-done((bf16[256,256]{1,0:T(8,128)(2,1)S(1)}, bf16[256,256]{1,0:T(8,128)(2,1)S(1)}, u32[]{:S(2)}, u32[]{:S(2)}) %collective-permute-start.24) | collective-permute-done | bytes 131104 | tf_op jit(solution)/shard_map/ppermute | solution.py:262
  114.4 4.3 %collective-permute-done.25.refs_3_ = bf16[256,256]{1,0:T(8,128)(2,1)S(1)} collective-permute-done((bf16[256,256]{1,0:T(8,128)(2,1)S(1)}, bf16[256,256]{1,0:T(8,128)(2,1)S(1)}, u32[]{:S(2)}, u32[]{:S(2)}) %collective-permute-start.25) | collective-permute-done | bytes 131104 | tf_op jit(solution)/shard_map/ppermute | solution.py:262
  118.8 1.3 collective-permute-start.26
  120.0 1.2 collective-permute-start.22
  121.2 4.5 %collective-permute-done.26.refs_4_ = bf16[512,256]{1,0:T(8,128)(2,1)S(1)} collective-permute-done((bf16[512,256]{1,0:T(8,128)(2,1)S(1)}, bf16[512,256]{1,0:T(8,128)(2,1)S(1)}, u32[]{:S(2)}, u32[]{:S(2)}) %collective-permute-start.26) | collective-permute-done | bytes 262176 | tf_op jit(solution)/shard_map/ppermute | solution.py:262
  125.7 1.9 %collective-permute-start.27 = (bf16[512,256]{1,0:T(8,128)(2,1)S(1)}, bf16[512,256]{1,0:T(8,128)(2,1)S(1)}, u32[]{:S(2)}, u32[]{:S(2)}) collective-permute-start(bf16[512,256]{1,0:T(8,128)(2,1)S(1)} %shard_map.79), channel_id=1, source_target_pairs={{0,1},{1,0},{2,3},{3,2},{4,5},{5,4},{6,7},{7,6},{8,9},{9,8},{10,11... | collective-permute-start | bytes 786440 | tf_op jit(solution)/shard_map/ppermute | solution.py:262
  127.6 1.2 collective-permute-start.19
  128.8 1.0 shard_map.80
  129.9 1.2 collective-permute-start.28
  131.1 4.3 %shard_map.76.refs_3_ = f32[512,2048]{1,0:T(8,128)S(1)} custom-call(s32[1]{0:T(128)} %bitcast.land_ref, bf16[512,128]{1,0:T(8,128)(2,1)S(1)} %get-tuple-element.37.refs_0_, bf16[512,384]{1,0:T(8,128)(2,1)S(1)} %get-tuple-element.42.refs_1_, bf16[2048,1024]{1,0:T(8,128)(2,1)S(1)} %copy-done), custom_call_target="tpu_custom_call" | custom-call | flops 1073741824 | bytes 8388608 | tf_op jit(solution)/shard_map/pallas_call | solution.py:427
  135.4 5.6 %shard_map.77 = f32[512,2048]{1,0:T(8,128)} custom-call(s32[1]{0:T(128)} %bitcast.land_ref, bf16[512,128]{1,0:T(8,128)(2,1)S(1)} %collective-permute-done.19.refs_0_, bf16[512,384]{1,0:T(8,128)(2,1)S(1)} %collective-permute-done.22.refs_1_, bf16[2048,1024]{1,0:T(8,128)(2,1)S(1)} %copy-done, f32[512,2048]{1,0:T(8,128)S(1)} %shard_map.76.refs_3_), custom_call_target="tpu_custom_call" | custom-call | flops 1073741824 | bytes 12582912 | tf_op jit(solution)/shard_map/pallas_call | solution.py:427
  141.0 1.1 shard_map.81
  (27 shorter events, 0.2 us)
Async XLA Ops:
  0.6 15.9 %collective-permute-start = (bf16[256,1280]{1,0:T(8,128)(2,1)}, bf16[256,1280]{1,0:T(8,128)(2,1)S(1)}, u32[]{:S(2)}, u32[]{:S(2)}) collective-permute-start(bf16[256,1280]{1,0:T(8,128)(2,1)} %refs_0_.1), channel_id=1, source_target_pairs={{0,16},{16,0},{1,17},{17,1},{2,18},{18,2},{3,19},{19,3},{4,20},{20... | collective-permute-start | bytes 1966088 | tf_op jit(solution)/shard_map/ppermute | solution.py:265
  1.9 50.8 %collective-permute-start.1 = (bf16[256,1280]{1,0:T(8,128)(2,1)}, bf16[256,1280]{1,0:T(8,128)(2,1)S(1)}, u32[]{:S(2)}, u32[]{:S(2)}) collective-permute-start(bf16[256,1280]{1,0:T(8,128)(2,1)} %refs_0_.1), channel_id=1, source_target_pairs={{0,1},{1,0},{2,3},{3,2},{4,5},{5,4},{6,7},{7,6},{8,9},{9,8},{10,11... | collective-permute-start | bytes 1966088 | tf_op jit(solution)/shard_map/ppermute | solution.py:262
  16.5 39.2 %collective-permute-start.2 = (bf16[256,1280]{1,0:T(8,128)(2,1)S(1)}, bf16[256,1280]{1,0:T(8,128)(2,1)S(1)}, u32[]{:S(2)}, u32[]{:S(2)}) collective-permute-start(bf16[256,1280]{1,0:T(8,128)(2,1)S(1)} %collective-permute-done.refs_1_), channel_id=1, source_target_pairs={{0,1},{1,0},{2,3},{3,2},{4,5},{5,4},{6,7},{7,6},{8,9},{9,8},{10,11... | collective-permute-start | bytes 1966088 | tf_op jit(solution)/shard_map/ppermute | solution.py:262
  18.1 5.3 %collective-permute-start.13 = (bf16[64,1024]{1,0:T(8,128)(2,1)}, bf16[64,1024]{1,0:T(8,128)(2,1)S(1)}, u32[]{:S(2)}, u32[]{:S(2)}) collective-permute-start(bf16[64,1024]{1,0:T(8,128)(2,1)} %refs_2_.3), channel_id=1, source_target_pairs={{0,2},{1,3},{2,0},{3,1},{4,6},{5,7},{6,4},{7,5},{8,10},{9,11},{10,... | collective-permute-start | bytes 393224 | tf_op jit(solution)/shard_map/ppermute | solution.py:262
  19.3 15.9 %collective-permute-start.4 = (bf16[64,1280]{1,0:T(8,128)(2,1)}, bf16[64,1280]{1,0:T(8,128)(2,1)S(1)}, u32[]{:S(2)}, u32[]{:S(2)}) collective-permute-start(bf16[64,1280]{1,0:T(8,128)(2,1)} %refs_1_.1), channel_id=1, source_target_pairs={{0,8},{1,9},{2,10},{3,11},{4,12},{5,13},{6,14},{7,15},{8,0},{9,1},... | collective-permute-start | bytes 491528 | tf_op jit(solution)/shard_map/ppermute | solution.py:262
  21.6 13.3 %collective-permute-start.11 = (bf16[64,1024]{1,0:T(8,128)(2,1)}, bf16[64,1024]{1,0:T(8,128)(2,1)S(1)}, u32[]{:S(2)}, u32[]{:S(2)}) collective-permute-start(bf16[64,1024]{1,0:T(8,128)(2,1)} %refs_2_.3), channel_id=1, source_target_pairs={{0,8},{1,9},{2,10},{3,11},{4,12},{5,13},{6,14},{7,15},{8,0},{9,1},... | collective-permute-start | bytes 393224 | tf_op jit(solution)/shard_map/ppermute | solution.py:262
  23.3 12.3 %collective-permute-start.3 = (bf16[64,1280]{1,0:T(8,128)(2,1)}, bf16[64,1280]{1,0:T(8,128)(2,1)S(1)}, u32[]{:S(2)}, u32[]{:S(2)}) collective-permute-start(bf16[64,1280]{1,0:T(8,128)(2,1)} %refs_1_.1), channel_id=1, source_target_pairs={{0,4},{1,5},{2,6},{3,7},{4,0},{5,1},{6,2},{7,3},{8,12},{9,13},{10,... | collective-permute-start | bytes 491528 | tf_op jit(solution)/shard_map/ppermute | solution.py:262
  34.9 5.5 %collective-permute-start.6 = (bf16[64,1280]{1,0:T(8,128)(2,1)}, bf16[64,1280]{1,0:T(8,128)(2,1)S(1)}, u32[]{:S(2)}, u32[]{:S(2)}) collective-permute-start(bf16[64,1280]{1,0:T(8,128)(2,1)} %refs_1_.1), channel_id=1, source_target_pairs={{0,2},{1,3},{2,0},{3,1},{4,6},{5,7},{6,4},{7,5},{8,10},{9,11},{10,... | collective-permute-start | bytes 491528 | tf_op jit(solution)/shard_map/ppermute | solution.py:262
  35.2 9.1 %collective-permute-start.5 = (bf16[64,1280]{1,0:T(8,128)(2,1)S(1)}, bf16[64,1280]{1,0:T(8,128)(2,1)S(1)}, u32[]{:S(2)}, u32[]{:S(2)}) collective-permute-start(bf16[64,1280]{1,0:T(8,128)(2,1)S(1)} %collective-permute-done.4.refs_6_), channel_id=1, source_target_pairs={{0,4},{1,5},{2,6},{3,7},{4,0},{5,1},{6,2},{7,3},{8,12},{9,13},{10,... | collective-permute-start | bytes 491528 | tf_op jit(solution)/shard_map/ppermute | solution.py:262
  35.6 7.4 %collective-permute-start.12 = (bf16[64,1024]{1,0:T(8,128)(2,1)S(1)}, bf16[64,1024]{1,0:T(8,128)(2,1)S(1)}, u32[]{:S(2)}, u32[]{:S(2)}) collective-permute-start(bf16[64,1024]{1,0:T(8,128)(2,1)S(1)} %collective-permute-done.11.refs_2_), channel_id=1, source_target_pairs={{0,4},{1,5},{2,6},{3,7},{4,0},{5,1},{6,2},{7,3},{8,12},{9,13},{10,... | collective-permute-start | bytes 393224 | tf_op jit(solution)/shard_map/ppermute | solution.py:262
  40.4 4.2 %collective-permute-start.7 = (bf16[64,1280]{1,0:T(8,128)(2,1)S(1)}, bf16[64,1280]{1,0:T(8,128)(2,1)S(1)}, u32[]{:S(2)}, u32[]{:S(2)}) collective-permute-start(bf16[64,1280]{1,0:T(8,128)(2,1)S(1)} %collective-permute-done.3.refs_5_), channel_id=1, source_target_pairs={{0,2},{1,3},{2,0},{3,1},{4,6},{5,7},{6,4},{7,5},{8,10},{9,11},{10,... | collective-permute-start | bytes 491528 | tf_op jit(solution)/shard_map/ppermute | solution.py:262
  43.0 6.1 %collective-permute-start.8 = (bf16[64,1280]{1,0:T(8,128)(2,1)S(1)}, bf16[64,1280]{1,0:T(8,128)(2,1)S(1)}, u32[]{:S(2)}, u32[]{:S(2)}) collective-permute-start(bf16[64,1280]{1,0:T(8,128)(2,1)S(1)} %collective-permute-done.4.refs_6_), channel_id=1, source_target_pairs={{0,2},{1,3},{2,0},{3,1},{4,6},{5,7},{6,4},{7,5},{8,10},{9,11},{10,... | collective-permute-start | bytes 491528 | tf_op jit(solution)/shard_map/ppermute | solution.py:262
  44.2 8.5 %collective-permute-start.9 = (bf16[64,1280]{1,0:T(8,128)(2,1)S(1)}, bf16[64,1280]{1,0:T(8,128)(2,1)S(1)}, u32[]{:S(2)}, u32[]{:S(2)}) collective-permute-start(bf16[64,1280]{1,0:T(8,128)(2,1)S(1)} %collective-permute-done.5.refs_7_), channel_id=1, source_target_pairs={{0,2},{1,3},{2,0},{3,1},{4,6},{5,7},{6,4},{7,5},{8,10},{9,11},{10,... | collective-permute-start | bytes 491528 | tf_op jit(solution)/shard_map/ppermute | solution.py:262
  44.6 13.2 %collective-permute-start.10 = (bf16[64,1024]{1,0:T(8,128)(2,1)}, bf16[64,1024]{1,0:T(8,128)(2,1)}, u32[]{:S(2)}, u32[]{:S(2)}) collective-permute-start(bf16[64,1024]{1,0:T(8,128)(2,1)} %refs_2_.3), channel_id=1, source_target_pairs={{0,4},{1,5},{2,6},{3,7},{4,0},{5,1},{6,2},{7,3},{8,12},{9,13},{10,... | collective-permute-start | bytes 393224 | tf_op jit(solution)/shard_map/ppermute | solution.py:262
  49.1 8.7 %collective-permute-start.15 = (bf16[64,1024]{1,0:T(8,128)(2,1)S(1)}, bf16[64,1024]{1,0:T(8,128)(2,1)}, u32[]{:S(2)}, u32[]{:S(2)}) collective-permute-start(bf16[64,1024]{1,0:T(8,128)(2,1)S(1)} %collective-permute-done.11.refs_2_), channel_id=1, source_target_pairs={{0,2},{1,3},{2,0},{3,1},{4,6},{5,7},{6,4},{7,5},{8,10},{9,11},{10,... | collective-permute-start | bytes 393224 | tf_op jit(solution)/shard_map/ppermute | solution.py:262
  52.7 5.0 %collective-permute-start.14 = (bf16[64,1024]{1,0:T(8,128)(2,1)S(1)}, bf16[64,1024]{1,0:T(8,128)(2,1)}, u32[]{:S(2)}, u32[]{:S(2)}) collective-permute-start(bf16[64,1024]{1,0:T(8,128)(2,1)S(1)} %collective-permute-done.13.refs_4_), channel_id=1, source_target_pairs={{0,4},{1,5},{2,6},{3,7},{4,0},{5,1},{6,2},{7,3},{8,12},{9,13},{10,... | collective-permute-start | bytes 393224 | tf_op jit(solution)/shard_map/ppermute | solution.py:262
  52.7 5.1 %collective-permute-start.16 = (bf16[64,1024]{1,0:T(8,128)(2,1)S(1)}, bf16[64,1024]{1,0:T(8,128)(2,1)}, u32[]{:S(2)}, u32[]{:S(2)}) collective-permute-start(bf16[64,1024]{1,0:T(8,128)(2,1)S(1)} %collective-permute-done.12.refs_3_), channel_id=1, source_target_pairs={{0,2},{1,3},{2,0},{3,1},{4,6},{5,7},{6,4},{7,5},{8,10},{9,11},{10,... | collective-permute-start | bytes 393224 | tf_op jit(solution)/shard_map/ppermute | solution.py:262
  52.7 1.1 copy-start.1
  53.8 0.9 copy-start.2
  54.8 0.9 copy-start.3
  60.8 8.4 %copy-start.4 = (s32[512]{0:T(512)S(1)}, s32[512]{0:T(512)}, u32[]{:S(2)}) copy-start(s32[512]{0:T(512)} %param.9) | copy-start | bytes 6148
  60.8 8.7 %collective-permute-start.20 = (bf16[512,768]{1,0:T(8,128)(2,1)}, bf16[512,768]{1,0:T(8,128)(2,1)S(1)}, u32[]{:S(2)}, u32[]{:S(2)}) collective-permute-start(bf16[512,768]{1,0:T(8,128)(2,1)} %get-tuple-element.39), channel_id=1, source_target_pairs={{0,1},{1,0},{2,3},{3,2},{4,5},{5,4},{6,7},{7,6},{8,9},{9,8},{10,11... | collective-permute-start | bytes 2359304 | tf_op jit(solution)/shard_map/ppermute | solution.py:262
  67.3 1.7 %collective-permute-start.17 = (bf16[512,256]{1,0:T(8,128)(2,1)}, bf16[512,256]{1,0:T(8,128)(2,1)S(1)}, u32[]{:S(2)}, u32[]{:S(2)}) collective-permute-start(bf16[512,256]{1,0:T(8,128)(2,1)} %get-tuple-element.31), channel_id=1, source_target_pairs={{0,1},{1,0},{2,3},{3,2},{4,5},{5,4},{6,7},{7,6},{8,9},{9,8},{10,11... | collective-permute-start | bytes 786440 | tf_op jit(solution)/shard_map/ppermute | solution.py:262
  69.6 10.6 %collective-permute-start.21 = (bf16[512,384]{1,0:T(8,128)(2,1)S(1)}, bf16[512,384]{1,0:T(8,128)(2,1)S(1)}, u32[]{:S(2)}, u32[]{:S(2)}) collective-permute-start(bf16[512,384]{1,0:T(8,128)(2,1)S(1)} %get-tuple-element.41), channel_id=1, source_target_pairs={{0,16},{16,0},{1,17},{17,1},{2,18},{18,2},{3,19},{19,3},{4,20},{20... | collective-permute-start | bytes 1179656 | tf_op jit(solution)/shard_map/ppermute | solution.py:265
  81.9 59.2 %all-to-all-start = ((bf16[32,32,384]{2,1,0:T(8,128)(2,1)}), bf16[32,32,384]{2,1,0:T(8,128)(2,1)S(1)}, u32[]{:S(2)}, u32[]{:S(2)}) async-start(bf16[32,32,384]{2,1,0:T(8,128)(2,1)} %bitcast.1), calls=%async_computation | async-start | bytes 1572864 | tf_op jit(solution)/shard_map/all_to_all | solution.py:412
  88.7 9.2 %collective-permute-start.18 = (bf16[512,128]{1,0:T(8,128)(2,1)S(1)}, bf16[512,128]{1,0:T(8,128)(2,1)S(1)}, u32[]{:S(2)}, u32[]{:S(2)}) collective-permute-start(bf16[512,128]{1,0:T(8,128)(2,1)S(1)} %get-tuple-element.33), channel_id=1, source_target_pairs={{0,16},{16,0},{1,17},{17,1},{2,18},{18,2},{3,19},{19,3},{4,20},{20... | collective-permute-start | bytes 393224 | tf_op jit(solution)/shard_map/ppermute | solution.py:265
  98.1 33.0 %copy-start = (bf16[2048,1024]{1,0:T(8,128)(2,1)S(1)}, bf16[2048,1024]{1,0:T(8,128)(2,1)}, u32[]{:S(2)}) copy-start(bf16[2048,1024]{1,0:T(8,128)(2,1)} %refs_2_.5) | copy-start | bytes 12582916
  98.8 6.1 %collective-permute-start.23 = (bf16[256,256]{1,0:T(8,128)(2,1)S(1)}, bf16[256,256]{1,0:T(8,128)(2,1)S(1)}, u32[]{:S(2)}, u32[]{:S(2)}) collective-permute-start(bf16[256,256]{1,0:T(8,128)(2,1)S(1)} %get-tuple-element.44), channel_id=1, source_target_pairs={{0,4},{1,5},{2,6},{3,7},{4,0},{5,1},{6,2},{7,3},{8,12},{9,13},{10,... | collective-permute-start | bytes 393224 | tf_op jit(solution)/shard_map/ppermute | solution.py:262
  100.3 14.1 %collective-permute-start.24 = (bf16[256,256]{1,0:T(8,128)(2,1)S(1)}, bf16[256,256]{1,0:T(8,128)(2,1)S(1)}, u32[]{:S(2)}, u32[]{:S(2)}) collective-permute-start(bf16[256,256]{1,0:T(8,128)(2,1)S(1)} %get-tuple-element.45), channel_id=1, source_target_pairs={{0,8},{1,9},{2,10},{3,11},{4,12},{5,13},{6,14},{7,15},{8,0},{9,1},... | collective-permute-start | bytes 393224 | tf_op jit(solution)/shard_map/ppermute | solution.py:262
  103.7 15.1 %collective-permute-start.25 = (bf16[256,256]{1,0:T(8,128)(2,1)S(1)}, bf16[256,256]{1,0:T(8,128)(2,1)S(1)}, u32[]{:S(2)}, u32[]{:S(2)}) collective-permute-start(bf16[256,256]{1,0:T(8,128)(2,1)S(1)} %get-tuple-element.46), channel_id=1, source_target_pairs={{0,12},{1,13},{2,14},{3,15},{4,8},{5,9},{6,10},{7,11},{8,4},{9,5},... | collective-permute-start | bytes 393224 | tf_op jit(solution)/shard_map/ppermute | solution.py:262
  118.8 7.0 %collective-permute-start.26 = (bf16[512,256]{1,0:T(8,128)(2,1)S(1)}, bf16[512,256]{1,0:T(8,128)(2,1)S(1)}, u32[]{:S(2)}, u32[]{:S(2)}) collective-permute-start(bf16[512,256]{1,0:T(8,128)(2,1)S(1)} %shard_map.78), channel_id=1, source_target_pairs={{0,2},{1,3},{2,0},{3,1},{4,6},{5,7},{6,4},{7,5},{8,10},{9,11},{10,... | collective-permute-start | bytes 786440 | tf_op jit(solution)/shard_map/ppermute | solution.py:262
  120.0 15.4 %collective-permute-start.22 = (bf16[512,384]{1,0:T(8,128)(2,1)S(1)}, bf16[512,384]{1,0:T(8,128)(2,1)S(1)}, u32[]{:S(2)}, u32[]{:S(2)}) collective-permute-start(bf16[512,384]{1,0:T(8,128)(2,1)S(1)} %get-tuple-element.42.refs_1_), channel_id=1, source_target_pairs={{0,16},{16,0},{1,17},{17,1},{2,18},{18,2},{3,19},{19,3},{4,20},{20... | collective-permute-start | bytes 1179656 | tf_op jit(solution)/shard_map/ppermute | solution.py:265
  125.7 3.1 %collective-permute-start.27 = (bf16[512,256]{1,0:T(8,128)(2,1)S(1)}, bf16[512,256]{1,0:T(8,128)(2,1)S(1)}, u32[]{:S(2)}, u32[]{:S(2)}) collective-permute-start(bf16[512,256]{1,0:T(8,128)(2,1)S(1)} %shard_map.79), channel_id=1, source_target_pairs={{0,1},{1,0},{2,3},{3,2},{4,5},{5,4},{6,7},{7,6},{8,9},{9,8},{10,11... | collective-permute-start | bytes 786440 | tf_op jit(solution)/shard_map/ppermute | solution.py:262
  127.6 7.8 %collective-permute-start.19 = (bf16[512,128]{1,0:T(8,128)(2,1)S(1)}, bf16[512,128]{1,0:T(8,128)(2,1)S(1)}, u32[]{:S(2)}, u32[]{:S(2)}) collective-permute-start(bf16[512,128]{1,0:T(8,128)(2,1)S(1)} %get-tuple-element.37.refs_0_), channel_id=1, source_target_pairs={{0,16},{16,0},{1,17},{17,1},{2,18},{18,2},{3,19},{19,3},{4,20},{20... | collective-permute-start | bytes 393224 | tf_op jit(solution)/shard_map/ppermute | solution.py:265
  129.9 11.1 %collective-permute-start.28 = (bf16[128,128]{1,0:T(8,128)(2,1)S(1)}, bf16[128,128]{1,0:T(8,128)(2,1)S(1)}, u32[]{:S(2)}, u32[]{:S(2)}) collective-permute-start(bf16[128,128]{1,0:T(8,128)(2,1)S(1)} %get-tuple-element.51), channel_id=1, source_target_pairs={{0,16},{16,0},{1,17},{17,1},{2,18},{18,2},{3,19},{19,3},{4,20},{20... | collective-permute-start | bytes 98312 | tf_op jit(solution)/shard_map/ppermute | solution.py:265

commit v3 on v2

--- a/solution.py
+++ b/solution.py
@@ -147,14 +147,16 @@
     own_ref, *sends, match_ref, count_ref, arrived, matched = refs
     take_body(plan, table_ref, *ins, arrived)
     slots, own_width = matched.shape
-    values = arrived[:, : own_ref.shape[1]]
-    tags = arrived[:, own_ref.shape[1] :].astype(jnp.float32)
+    width = own_ref.shape[1]
+    tags = arrived[:, width:].astype(jnp.float32)
     lane = lax.broadcasted_iota(jnp.int32, (slots, own_width), 1).astype(jnp.float32)
-    ones = jnp.ones((slots, own_width), jnp.bfloat16)
+    arrived[:, width:] = jnp.ones((slots, own_width), jnp.bfloat16)
+    values = arrived[...]
     for s, out in enumerate([own_ref, *sends]):
         match = (tags == lane + (1 + s * own_width)).astype(jnp.float32).astype(jnp.bfloat16)
-        counts = over_slots(match, ones)
-        out[...] = (over_slots(match, values) / jnp.maximum(counts, 1.0)).astype(out.dtype)
+        sums = over_slots(match, values)
+        counts = sums[:, width:]
+        out[...] = (sums[:, :width] / jnp.maximum(counts, 1.0)).astype(out.dtype)
         if s == 0:
             matched[...] = match
             count_ref[...] = counts

time: 142 us -> 142 us (level)
  no operation moved by 1% of the time
where the time goes in v3:
time: 142 us
  waiting for transfers between devices  79 us (56%)
  starting transfers between devices  35.8 us (25%)
  Pallas kernels  22.2 us (16%)
  local copies, waits for them, and re-layouts  3.04 us (2%)
    ppermute x23, waiting for transfers between devices, move(): return lax.ppermute(x, 'dp', axis_perm(sizes, axis, step))  48.8 us
    ppermute x6, waiting for transfers between devices, land_send(): lax.ppermute(x, 'land', [(s, (s + step) % land_count) for s in range(land...  30.2 us
    ppermute x23, starting transfers between devices, move(): return lax.ppermute(x, 'dp', axis_perm(sizes, axis, step))  21.7 us
    pallas_call x12, Pallas kernels, call(): pl.pallas_call(body, out_shape=list(outs), in_specs=[SMEM] + [VMEM] * len...  12.3 us
    pallas_call x2, Pallas kernels, by_block(): pl.pallas_call(functools.partial(body, land_count, parts), grid=(cent_blo...  9.89 us
    ppermute x6, starting transfers between devices, land_send(): lax.ppermute(x, 'land', [(s, (s + step) % land_count) for s in range(land...  7.26 us
    all_to_all x1, starting transfers between devices, local(): lax.all_to_all(outgoing.reshape(land_count * dp_count, slot_count, widths...  6.84 us
    unnamed x10, local copies, waits for them, and re-layouts  2.91 us
  transfers between devices with their start and end apart: 30, of which 15 were waited for; matrix products, arithmetic and copies ran while one was open for 1% of the time, Pallas kernels for 11%

profile of v3, /device:TPU:9, one launch (start us, length us, event | category | flops | bytes accessed | tf_op | source)
XLA Modules:
  0.0 142.1 jit_solution(15518495033009999196)
XLA Ops:
  0.6 1.3 collective-permute-start
  1.9 1.0 collective-permute-start.1
  2.9 13.7 %collective-permute-done.refs_1_ = bf16[256,1280]{1,0:T(8,128)(2,1)S(1)} collective-permute-done((bf16[256,1280]{1,0:T(8,128)(2,1)}, bf16[256,1280]{1,0:T(8,128)(2,1)S(1)}, u32[]{:S(2)}, u32[]{:S(2)}) %collective-permute-start) | collective-permute-done | bytes 655392 | tf_op jit(solution)/shard_map/ppermute | solution.py:267
  16.5 1.5 %collective-permute-start.2 = (bf16[256,1280]{1,0:T(8,128)(2,1)S(1)}, bf16[256,1280]{1,0:T(8,128)(2,1)S(1)}, u32[]{:S(2)}, u32[]{:S(2)}) collective-permute-start(bf16[256,1280]{1,0:T(8,128)(2,1)S(1)} %collective-permute-done.refs_1_), channel_id=1, source_target_pairs={{0,1},{1,0},{2,3},{3,2},{4,5},{5,4},{6,7},{7,6},{8,9},{9,8},{10,11... | collective-permute-start | bytes 1966088 | tf_op jit(solution)/shard_map/ppermute | solution.py:264
  18.1 1.2 collective-permute-start.13
  19.3 2.3 %collective-permute-start.4 = (bf16[64,1280]{1,0:T(8,128)(2,1)}, bf16[64,1280]{1,0:T(8,128)(2,1)S(1)}, u32[]{:S(2)}, u32[]{:S(2)}) collective-permute-start(bf16[64,1280]{1,0:T(8,128)(2,1)} %refs_1_.1), channel_id=1, source_target_pairs={{0,8},{1,9},{2,10},{3,11},{4,12},{5,13},{6,14},{7,15},{8,0},{9,1},... | collective-permute-start | bytes 491528 | tf_op jit(solution)/shard_map/ppermute | solution.py:264
  21.6 0.1 collective-permute-start.11
  21.7 1.7 %collective-permute-done.13.refs_4_ = bf16[64,1024]{1,0:T(8,128)(2,1)S(1)} collective-permute-done((bf16[64,1024]{1,0:T(8,128)(2,1)}, bf16[64,1024]{1,0:T(8,128)(2,1)S(1)}, u32[]{:S(2)}, u32[]{:S(2)}) %collective-permute-start.13) | collective-permute-done | bytes 131104 | tf_op jit(solution)/shard_map/ppermute | solution.py:264
  23.3 0.0 collective-permute-start.3
  23.3 11.6 %collective-permute-done.11.refs_2_ = bf16[64,1024]{1,0:T(8,128)(2,1)S(1)} collective-permute-done((bf16[64,1024]{1,0:T(8,128)(2,1)}, bf16[64,1024]{1,0:T(8,128)(2,1)S(1)}, u32[]{:S(2)}, u32[]{:S(2)}) %collective-permute-start.11) | collective-permute-done | bytes 131104 | tf_op jit(solution)/shard_map/ppermute | solution.py:264
  34.9 0.2 collective-permute-start.6
  35.2 0.0 collective-permute-done.4.refs_6_
  35.2 0.4 collective-permute-start.5
  35.6 0.0 collective-permute-done.3.refs_5_
  35.6 1.0 collective-permute-start.12
  36.6 3.8 %collective-permute-done.6.refs_8_ = bf16[64,1280]{1,0:T(8,128)(2,1)S(1)} collective-permute-done((bf16[64,1280]{1,0:T(8,128)(2,1)}, bf16[64,1280]{1,0:T(8,128)(2,1)S(1)}, u32[]{:S(2)}, u32[]{:S(2)}) %collective-permute-start.6) | collective-permute-done | bytes 163872 | tf_op jit(solution)/shard_map/ppermute | solution.py:264
  40.4 0.2 collective-permute-start.7
  40.7 2.3 %collective-permute-done.12.refs_3_ = bf16[64,1024]{1,0:T(8,128)(2,1)S(1)} collective-permute-done((bf16[64,1024]{1,0:T(8,128)(2,1)S(1)}, bf16[64,1024]{1,0:T(8,128)(2,1)S(1)}, u32[]{:S(2)}, u32[]{:S(2)}) %collective-permute-start.12) | collective-permute-done | bytes 131104 | tf_op jit(solution)/shard_map/ppermute | solution.py:264
  43.0 1.2 collective-permute-start.8
  44.2 0.2 collective-permute-start.9
  44.5 0.1 collective-permute-done.7.refs_9_
  44.6 0.0 collective-permute-start.10
  44.6 4.5 %collective-permute-done.8.refs_10_ = bf16[64,1280]{1,0:T(8,128)(2,1)S(1)} collective-permute-done((bf16[64,1280]{1,0:T(8,128)(2,1)S(1)}, bf16[64,1280]{1,0:T(8,128)(2,1)S(1)}, u32[]{:S(2)}, u32[]{:S(2)}) %collective-permute-start.8) | collective-permute-done | bytes 163872 | tf_op jit(solution)/shard_map/ppermute | solution.py:264
  49.1 3.6 %collective-permute-done.9.refs_11_ = bf16[64,1280]{1,0:T(8,128)(2,1)S(1)} collective-permute-done((bf16[64,1280]{1,0:T(8,128)(2,1)S(1)}, bf16[64,1280]{1,0:T(8,128)(2,1)S(1)}, u32[]{:S(2)}, u32[]{:S(2)}) %collective-permute-start.9) | collective-permute-done | bytes 163872 | tf_op jit(solution)/shard_map/ppermute | solution.py:264
  52.8 1.1 copy-done.1
  53.8 0.9 copy-done.2
  54.8 0.9 copy-done.3
  55.7 0.1 shard_map.68
  55.7 2.0 %shard_map.69.kern_ref = bf16[1024,512]{1,0:T(8,128)(2,1)S(1)} custom-call(s32[1]{0:T(128)} %bitcast.land_ref, bf16[256,1280]{1,0:T(8,128)(2,1)S(1)} %get-tuple-element.27.refs_0_, bf16[256,1280]{1,0:T(8,128)(2,1)S(1)} %collective-permute-done.refs_1_, bf16[256,1280]{1,0:T(8,128)(2,1)S(1)} %collective-permute-done.1.refs_2_, ...), custom_call_target="tpu_custom_call" | custom-call | flops 1342177280 | bytes 4980736 | tf_op jit(solution)/shard_map/pallas_call | solution.py:46
  57.8 3.0 %shard_map.73 = (f32[512,768]{1,0:T(8,128)S(1)}, bf16[512,768]{1,0:T(8,128)(2,1)}) custom-call(s32[1]{0:T(128)} %bitcast.land_ref, bf16[1024,512]{1,0:T(8,128)(2,1)S(1)} %shard_map.69.kern_ref, bf16[64,1024]{1,0:T(8,128)(2,1)S(1)} %get-tuple-element.29.refs_0_, bf16[64,1024]{1,0:T(8,128)(2,1)} %collective-permute-done.10.refs_1_, ...), custom_call_target="tpu_custom_call" | custom-call | flops 805306368 | bytes 4456448 | tf_op jit(solution)/shard_map/pallas_call | solution.py:46
  60.8 4.0 %collective-permute-start.20 = (bf16[512,768]{1,0:T(8,128)(2,1)}, bf16[512,768]{1,0:T(8,128)(2,1)S(1)}, u32[]{:S(2)}, u32[]{:S(2)}) collective-permute-start(bf16[512,768]{1,0:T(8,128)(2,1)} %get-tuple-element.39), channel_id=1, source_target_pairs={{0,1},{1,0},{2,3},{3,2},{4,5},{5,4},{6,7},{7,6},{8,9},{9,8},{10,11... | collective-permute-start | bytes 2359304 | tf_op jit(solution)/shard_map/ppermute | solution.py:264
  64.8 2.5 %shard_map.70 = (f32[512,256]{1,0:T(8,128)S(1)}, bf16[512,256]{1,0:T(8,128)(2,1)}) custom-call(s32[1]{0:T(128)} %bitcast.land_ref, bf16[1024,512]{1,0:T(8,128)(2,1)S(1)} %shard_map.69.kern_ref, bf16[64,1024]{1,0:T(8,128)(2,1)S(1)} %get-tuple-element.29.refs_0_, bf16[64,1024]{1,0:T(8,128)(2,1)} %collective-permute-done.10.refs_1_, ...), custom_call_target="tpu_custom_call" | custom-call | flops 268435456 | bytes 2883584 | tf_op jit(solution)/shard_map/pallas_call | solution.py:46
  67.3 0.0 collective-permute-start.17
  67.3 1.7 %collective-permute-done.17.refs_1_ = bf16[512,256]{1,0:T(8,128)(2,1)S(1)} collective-permute-done((bf16[512,256]{1,0:T(8,128)(2,1)}, bf16[512,256]{1,0:T(8,128)(2,1)S(1)}, u32[]{:S(2)}, u32[]{:S(2)}) %collective-permute-start.17) | collective-permute-done | bytes 262176 | tf_op jit(solution)/shard_map/ppermute | solution.py:264
  69.1 0.1 shard_map.71
  69.2 0.2 convert_reduce_fusion
  69.5 0.1 shard_map.74
  69.6 1.1 collective-permute-start.21
  70.8 0.4 fusion.1.refs_2_
  71.2 9.0 %collective-permute-done.21.refs_1_ = bf16[512,384]{1,0:T(8,128)(2,1)S(1)} collective-permute-done((bf16[512,384]{1,0:T(8,128)(2,1)S(1)}, bf16[512,384]{1,0:T(8,128)(2,1)S(1)}, u32[]{:S(2)}, u32[]{:S(2)}) %collective-permute-start.21) | collective-permute-done | bytes 393248 | tf_op jit(solution)/shard_map/ppermute | solution.py:267
  80.2 1.6 %shard_map.75 = (bf16[512,384]{1,0:T(8,128)(2,1)S(1)}, bf16[1024,384]{1,0:T(8,128)(2,1)}) custom-call(s32[1]{0:T(128)} %bitcast.land_ref, bf16[512,384]{1,0:T(8,128)(2,1)S(1)} %get-tuple-element.40.refs_0_, bf16[512,384]{1,0:T(8,128)(2,1)S(1)} %collective-permute-done.21.refs_1_, bf16[1024,512]{1,0:T(8,128)(2,1)S(1)} %fusion.1.refs_2_), custom_call_target="tpu_custom_call" | custom-call | flops 402653184 | bytes 3014656 | tf_op jit(solution)/shard_map/pallas_call | solution.py:46
  81.9 6.8 %all-to-all-start = ((bf16[32,32,384]{2,1,0:T(8,128)(2,1)}), bf16[32,32,384]{2,1,0:T(8,128)(2,1)S(1)}, u32[]{:S(2)}, u32[]{:S(2)}) async-start(bf16[32,32,384]{2,1,0:T(8,128)(2,1)} %bitcast.1), calls=%async_computation | async-start | bytes 1572864 | tf_op jit(solution)/shard_map/all_to_all | solution.py:414
  88.7 1.2 collective-permute-start.18
  90.0 0.4 fusion.refs_2_
  90.4 7.6 %collective-permute-done.18.refs_1_ = bf16[512,128]{1,0:T(8,128)(2,1)S(1)} collective-permute-done((bf16[512,128]{1,0:T(8,128)(2,1)S(1)}, bf16[512,128]{1,0:T(8,128)(2,1)S(1)}, u32[]{:S(2)}, u32[]{:S(2)}) %collective-permute-start.18) | collective-permute-done | bytes 131104 | tf_op jit(solution)/shard_map/ppermute | solution.py:267
  97.9 0.1 broadcast_in_dim.2.refs_3_
  98.1 0.0 copy-start
  98.1 0.7 shard_map.72
  98.8 1.5 %collective-permute-start.23 = (bf16[256,256]{1,0:T(8,128)(2,1)S(1)}, bf16[256,256]{1,0:T(8,128)(2,1)S(1)}, u32[]{:S(2)}, u32[]{:S(2)}) collective-permute-start(bf16[256,256]{1,0:T(8,128)(2,1)S(1)} %get-tuple-element.44), channel_id=1, source_target_pairs={{0,4},{1,5},{2,6},{3,7},{4,0},{5,1},{6,2},{7,3},{8,12},{9,13},{10,... | collective-permute-start | bytes 393224 | tf_op jit(solution)/shard_map/ppermute | solution.py:264
  100.3 3.4 %collective-permute-start.24 = (bf16[256,256]{1,0:T(8,128)(2,1)S(1)}, bf16[256,256]{1,0:T(8,128)(2,1)S(1)}, u32[]{:S(2)}, u32[]{:S(2)}) collective-permute-start(bf16[256,256]{1,0:T(8,128)(2,1)S(1)} %get-tuple-element.45), channel_id=1, source_target_pairs={{0,8},{1,9},{2,10},{3,11},{4,12},{5,13},{6,14},{7,15},{8,0},{9,1},... | collective-permute-start | bytes 393224 | tf_op jit(solution)/shard_map/ppermute | solution.py:264
  103.7 0.2 collective-permute-start.25
  103.9 1.1 collective-permute-done.23.refs_1_
  104.9 9.5 %collective-permute-done.24.refs_2_ = bf16[256,256]{1,0:T(8,128)(2,1)S(1)} collective-permute-done((bf16[256,256]{1,0:T(8,128)(2,1)S(1)}, bf16[256,256]{1,0:T(8,128)(2,1)S(1)}, u32[]{:S(2)}, u32[]{:S(2)}) %collective-permute-start.24) | collective-permute-done | bytes 131104 | tf_op jit(solution)/shard_map/ppermute | solution.py:264
  114.4 4.3 %collective-permute-done.25.refs_3_ = bf16[256,256]{1,0:T(8,128)(2,1)S(1)} collective-permute-done((bf16[256,256]{1,0:T(8,128)(2,1)S(1)}, bf16[256,256]{1,0:T(8,128)(2,1)S(1)}, u32[]{:S(2)}, u32[]{:S(2)}) %collective-permute-start.25) | collective-permute-done | bytes 131104 | tf_op jit(solution)/shard_map/ppermute | solution.py:264
  118.8 1.3 collective-permute-start.26
  120.0 1.2 collective-permute-start.22
  121.2 4.5 %collective-permute-done.26.refs_4_ = bf16[512,256]{1,0:T(8,128)(2,1)S(1)} collective-permute-done((bf16[512,256]{1,0:T(8,128)(2,1)S(1)}, bf16[512,256]{1,0:T(8,128)(2,1)S(1)}, u32[]{:S(2)}, u32[]{:S(2)}) %collective-permute-start.26) | collective-permute-done | bytes 262176 | tf_op jit(solution)/shard_map/ppermute | solution.py:264
  125.7 1.9 %collective-permute-start.27 = (bf16[512,256]{1,0:T(8,128)(2,1)S(1)}, bf16[512,256]{1,0:T(8,128)(2,1)S(1)}, u32[]{:S(2)}, u32[]{:S(2)}) collective-permute-start(bf16[512,256]{1,0:T(8,128)(2,1)S(1)} %shard_map.79), channel_id=1, source_target_pairs={{0,1},{1,0},{2,3},{3,2},{4,5},{5,4},{6,7},{7,6},{8,9},{9,8},{10,11... | collective-permute-start | bytes 786440 | tf_op jit(solution)/shard_map/ppermute | solution.py:264
  127.6 1.2 collective-permute-start.19
  128.8 0.9 shard_map.80
  129.8 1.2 collective-permute-start.28
  131.0 4.3 %shard_map.76.refs_3_ = f32[512,2048]{1,0:T(8,128)S(1)} custom-call(s32[1]{0:T(128)} %bitcast.land_ref, bf16[512,128]{1,0:T(8,128)(2,1)S(1)} %get-tuple-element.37.refs_0_, bf16[512,384]{1,0:T(8,128)(2,1)S(1)} %get-tuple-element.42.refs_1_, bf16[2048,1024]{1,0:T(8,128)(2,1)S(1)} %copy-done), custom_call_target="tpu_custom_call" | custom-call | flops 1073741824 | bytes 8388608 | tf_op jit(solution)/shard_map/pallas_call | solution.py:429
  135.3 5.6 %shard_map.77 = f32[512,2048]{1,0:T(8,128)} custom-call(s32[1]{0:T(128)} %bitcast.land_ref, bf16[512,128]{1,0:T(8,128)(2,1)S(1)} %collective-permute-done.19.refs_0_, bf16[512,384]{1,0:T(8,128)(2,1)S(1)} %collective-permute-done.22.refs_1_, bf16[2048,1024]{1,0:T(8,128)(2,1)S(1)} %copy-done, f32[512,2048]{1,0:T(8,128)S(1)} %shard_map.76.refs_3_), custom_call_target="tpu_custom_call" | custom-call | flops 1073741824 | bytes 12582912 | tf_op jit(solution)/shard_map/pallas_call | solution.py:429
  140.9 1.1 shard_map.81
  (27 shorter events, 0.2 us)
Async XLA Ops:
  0.6 15.9 %collective-permute-start = (bf16[256,1280]{1,0:T(8,128)(2,1)}, bf16[256,1280]{1,0:T(8,128)(2,1)S(1)}, u32[]{:S(2)}, u32[]{:S(2)}) collective-permute-start(bf16[256,1280]{1,0:T(8,128)(2,1)} %refs_0_.1), channel_id=1, source_target_pairs={{0,16},{16,0},{1,17},{17,1},{2,18},{18,2},{3,19},{19,3},{4,20},{20... | collective-permute-start | bytes 1966088 | tf_op jit(solution)/shard_map/ppermute | solution.py:267
  1.9 50.8 %collective-permute-start.1 = (bf16[256,1280]{1,0:T(8,128)(2,1)}, bf16[256,1280]{1,0:T(8,128)(2,1)S(1)}, u32[]{:S(2)}, u32[]{:S(2)}) collective-permute-start(bf16[256,1280]{1,0:T(8,128)(2,1)} %refs_0_.1), channel_id=1, source_target_pairs={{0,1},{1,0},{2,3},{3,2},{4,5},{5,4},{6,7},{7,6},{8,9},{9,8},{10,11... | collective-permute-start | bytes 1966088 | tf_op jit(solution)/shard_map/ppermute | solution.py:264
  16.5 39.2 %collective-permute-start.2 = (bf16[256,1280]{1,0:T(8,128)(2,1)S(1)}, bf16[256,1280]{1,0:T(8,128)(2,1)S(1)}, u32[]{:S(2)}, u32[]{:S(2)}) collective-permute-start(bf16[256,1280]{1,0:T(8,128)(2,1)S(1)} %collective-permute-done.refs_1_), channel_id=1, source_target_pairs={{0,1},{1,0},{2,3},{3,2},{4,5},{5,4},{6,7},{7,6},{8,9},{9,8},{10,11... | collective-permute-start | bytes 1966088 | tf_op jit(solution)/shard_map/ppermute | solution.py:264
  18.1 5.3 %collective-permute-start.13 = (bf16[64,1024]{1,0:T(8,128)(2,1)}, bf16[64,1024]{1,0:T(8,128)(2,1)S(1)}, u32[]{:S(2)}, u32[]{:S(2)}) collective-permute-start(bf16[64,1024]{1,0:T(8,128)(2,1)} %refs_2_.3), channel_id=1, source_target_pairs={{0,2},{1,3},{2,0},{3,1},{4,6},{5,7},{6,4},{7,5},{8,10},{9,11},{10,... | collective-permute-start | bytes 393224 | tf_op jit(solution)/shard_map/ppermute | solution.py:264
  19.3 15.9 %collective-permute-start.4 = (bf16[64,1280]{1,0:T(8,128)(2,1)}, bf16[64,1280]{1,0:T(8,128)(2,1)S(1)}, u32[]{:S(2)}, u32[]{:S(2)}) collective-permute-start(bf16[64,1280]{1,0:T(8,128)(2,1)} %refs_1_.1), channel_id=1, source_target_pairs={{0,8},{1,9},{2,10},{3,11},{4,12},{5,13},{6,14},{7,15},{8,0},{9,1},... | collective-permute-start | bytes 491528 | tf_op jit(solution)/shard_map/ppermute | solution.py:264
  21.6 13.3 %collective-permute-start.11 = (bf16[64,1024]{1,0:T(8,128)(2,1)}, bf16[64,1024]{1,0:T(8,128)(2,1)S(1)}, u32[]{:S(2)}, u32[]{:S(2)}) collective-permute-start(bf16[64,1024]{1,0:T(8,128)(2,1)} %refs_2_.3), channel_id=1, source_target_pairs={{0,8},{1,9},{2,10},{3,11},{4,12},{5,13},{6,14},{7,15},{8,0},{9,1},... | collective-permute-start | bytes 393224 | tf_op jit(solution)/shard_map/ppermute | solution.py:264
  23.3 12.3 %collective-permute-start.3 = (bf16[64,1280]{1,0:T(8,128)(2,1)}, bf16[64,1280]{1,0:T(8,128)(2,1)S(1)}, u32[]{:S(2)}, u32[]{:S(2)}) collective-permute-start(bf16[64,1280]{1,0:T(8,128)(2,1)} %refs_1_.1), channel_id=1, source_target_pairs={{0,4},{1,5},{2,6},{3,7},{4,0},{5,1},{6,2},{7,3},{8,12},{9,13},{10,... | collective-permute-start | bytes 491528 | tf_op jit(solution)/shard_map/ppermute | solution.py:264
  34.9 5.5 %collective-permute-start.6 = (bf16[64,1280]{1,0:T(8,128)(2,1)}, bf16[64,1280]{1,0:T(8,128)(2,1)S(1)}, u32[]{:S(2)}, u32[]{:S(2)}) collective-permute-start(bf16[64,1280]{1,0:T(8,128)(2,1)} %refs_1_.1), channel_id=1, source_target_pairs={{0,2},{1,3},{2,0},{3,1},{4,6},{5,7},{6,4},{7,5},{8,10},{9,11},{10,... | collective-permute-start | bytes 491528 | tf_op jit(solution)/shard_map/ppermute | solution.py:264
  35.2 9.1 %collective-permute-start.5 = (bf16[64,1280]{1,0:T(8,128)(2,1)S(1)}, bf16[64,1280]{1,0:T(8,128)(2,1)S(1)}, u32[]{:S(2)}, u32[]{:S(2)}) collective-permute-start(bf16[64,1280]{1,0:T(8,128)(2,1)S(1)} %collective-permute-done.4.refs_6_), channel_id=1, source_target_pairs={{0,4},{1,5},{2,6},{3,7},{4,0},{5,1},{6,2},{7,3},{8,12},{9,13},{10,... | collective-permute-start | bytes 491528 | tf_op jit(solution)/shard_map/ppermute | solution.py:264
  35.6 7.4 %collective-permute-start.12 = (bf16[64,1024]{1,0:T(8,128)(2,1)S(1)}, bf16[64,1024]{1,0:T(8,128)(2,1)S(1)}, u32[]{:S(2)}, u32[]{:S(2)}) collective-permute-start(bf16[64,1024]{1,0:T(8,128)(2,1)S(1)} %collective-permute-done.11.refs_2_), channel_id=1, source_target_pairs={{0,4},{1,5},{2,6},{3,7},{4,0},{5,1},{6,2},{7,3},{8,12},{9,13},{10,... | collective-permute-start | bytes 393224 | tf_op jit(solution)/shard_map/ppermute | solution.py:264
  40.4 4.2 %collective-permute-start.7 = (bf16[64,1280]{1,0:T(8,128)(2,1)S(1)}, bf16[64,1280]{1,0:T(8,128)(2,1)S(1)}, u32[]{:S(2)}, u32[]{:S(2)}) collective-permute-start(bf16[64,1280]{1,0:T(8,128)(2,1)S(1)} %collective-permute-done.3.refs_5_), channel_id=1, source_target_pairs={{0,2},{1,3},{2,0},{3,1},{4,6},{5,7},{6,4},{7,5},{8,10},{9,11},{10,... | collective-permute-start | bytes 491528 | tf_op jit(solution)/shard_map/ppermute | solution.py:264
  43.0 6.1 %collective-permute-start.8 = (bf16[64,1280]{1,0:T(8,128)(2,1)S(1)}, bf16[64,1280]{1,0:T(8,128)(2,1)S(1)}, u32[]{:S(2)}, u32[]{:S(2)}) collective-permute-start(bf16[64,1280]{1,0:T(8,128)(2,1)S(1)} %collective-permute-done.4.refs_6_), channel_id=1, source_target_pairs={{0,2},{1,3},{2,0},{3,1},{4,6},{5,7},{6,4},{7,5},{8,10},{9,11},{10,... | collective-permute-start | bytes 491528 | tf_op jit(solution)/shard_map/ppermute | solution.py:264
  44.2 8.5 %collective-permute-start.9 = (bf16[64,1280]{1,0:T(8,128)(2,1)S(1)}, bf16[64,1280]{1,0:T(8,128)(2,1)S(1)}, u32[]{:S(2)}, u32[]{:S(2)}) collective-permute-start(bf16[64,1280]{1,0:T(8,128)(2,1)S(1)} %collective-permute-done.5.refs_7_), channel_id=1, source_target_pairs={{0,2},{1,3},{2,0},{3,1},{4,6},{5,7},{6,4},{7,5},{8,10},{9,11},{10,... | collective-permute-start | bytes 491528 | tf_op jit(solution)/shard_map/ppermute | solution.py:264
  44.6 13.2 %collective-permute-start.10 = (bf16[64,1024]{1,0:T(8,128)(2,1)}, bf16[64,1024]{1,0:T(8,128)(2,1)}, u32[]{:S(2)}, u32[]{:S(2)}) collective-permute-start(bf16[64,1024]{1,0:T(8,128)(2,1)} %refs_2_.3), channel_id=1, source_target_pairs={{0,4},{1,5},{2,6},{3,7},{4,0},{5,1},{6,2},{7,3},{8,12},{9,13},{10,... | collective-permute-start | bytes 393224 | tf_op jit(solution)/shard_map/ppermute | solution.py:264
  49.1 8.7 %collective-permute-start.15 = (bf16[64,1024]{1,0:T(8,128)(2,1)S(1)}, bf16[64,1024]{1,0:T(8,128)(2,1)}, u32[]{:S(2)}, u32[]{:S(2)}) collective-permute-start(bf16[64,1024]{1,0:T(8,128)(2,1)S(1)} %collective-permute-done.11.refs_2_), channel_id=1, source_target_pairs={{0,2},{1,3},{2,0},{3,1},{4,6},{5,7},{6,4},{7,5},{8,10},{9,11},{10,... | collective-permute-start | bytes 393224 | tf_op jit(solution)/shard_map/ppermute | solution.py:264
  52.7 5.0 %collective-permute-start.14 = (bf16[64,1024]{1,0:T(8,128)(2,1)S(1)}, bf16[64,1024]{1,0:T(8,128)(2,1)}, u32[]{:S(2)}, u32[]{:S(2)}) collective-permute-start(bf16[64,1024]{1,0:T(8,128)(2,1)S(1)} %collective-permute-done.13.refs_4_), channel_id=1, source_target_pairs={{0,4},{1,5},{2,6},{3,7},{4,0},{5,1},{6,2},{7,3},{8,12},{9,13},{10,... | collective-permute-start | bytes 393224 | tf_op jit(solution)/shard_map/ppermute | solution.py:264
  52.7 5.1 %collective-permute-start.16 = (bf16[64,1024]{1,0:T(8,128)(2,1)S(1)}, bf16[64,1024]{1,0:T(8,128)(2,1)}, u32[]{:S(2)}, u32[]{:S(2)}) collective-permute-start(bf16[64,1024]{1,0:T(8,128)(2,1)S(1)} %collective-permute-done.12.refs_3_), channel_id=1, source_target_pairs={{0,2},{1,3},{2,0},{3,1},{4,6},{5,7},{6,4},{7,5},{8,10},{9,11},{10,... | collective-permute-start | bytes 393224 | tf_op jit(solution)/shard_map/ppermute | solution.py:264
  52.7 1.1 copy-start.1
  53.8 0.9 copy-start.2
  54.8 0.9 copy-start.3
  60.8 8.4 %copy-start.4 = (s32[512]{0:T(512)S(1)}, s32[512]{0:T(512)}, u32[]{:S(2)}) copy-start(s32[512]{0:T(512)} %param.9) | copy-start | bytes 6148
  60.8 8.7 %collective-permute-start.20 = (bf16[512,768]{1,0:T(8,128)(2,1)}, bf16[512,768]{1,0:T(8,128)(2,1)S(1)}, u32[]{:S(2)}, u32[]{:S(2)}) collective-permute-start(bf16[512,768]{1,0:T(8,128)(2,1)} %get-tuple-element.39), channel_id=1, source_target_pairs={{0,1},{1,0},{2,3},{3,2},{4,5},{5,4},{6,7},{7,6},{8,9},{9,8},{10,11... | collective-permute-start | bytes 2359304 | tf_op jit(solution)/shard_map/ppermute | solution.py:264
  67.3 1.7 %collective-permute-start.17 = (bf16[512,256]{1,0:T(8,128)(2,1)}, bf16[512,256]{1,0:T(8,128)(2,1)S(1)}, u32[]{:S(2)}, u32[]{:S(2)}) collective-permute-start(bf16[512,256]{1,0:T(8,128)(2,1)} %get-tuple-element.31), channel_id=1, source_target_pairs={{0,1},{1,0},{2,3},{3,2},{4,5},{5,4},{6,7},{7,6},{8,9},{9,8},{10,11... | collective-permute-start | bytes 786440 | tf_op jit(solution)/shard_map/ppermute | solution.py:264
  69.6 10.6 %collective-permute-start.21 = (bf16[512,384]{1,0:T(8,128)(2,1)S(1)}, bf16[512,384]{1,0:T(8,128)(2,1)S(1)}, u32[]{:S(2)}, u32[]{:S(2)}) collective-permute-start(bf16[512,384]{1,0:T(8,128)(2,1)S(1)} %get-tuple-element.41), channel_id=1, source_target_pairs={{0,16},{16,0},{1,17},{17,1},{2,18},{18,2},{3,19},{19,3},{4,20},{20... | collective-permute-start | bytes 1179656 | tf_op jit(solution)/shard_map/ppermute | solution.py:267
  81.9 59.1 %all-to-all-start = ((bf16[32,32,384]{2,1,0:T(8,128)(2,1)}), bf16[32,32,384]{2,1,0:T(8,128)(2,1)S(1)}, u32[]{:S(2)}, u32[]{:S(2)}) async-start(bf16[32,32,384]{2,1,0:T(8,128)(2,1)} %bitcast.1), calls=%async_computation | async-start | bytes 1572864 | tf_op jit(solution)/shard_map/all_to_all | solution.py:414
  88.7 9.2 %collective-permute-start.18 = (bf16[512,128]{1,0:T(8,128)(2,1)S(1)}, bf16[512,128]{1,0:T(8,128)(2,1)S(1)}, u32[]{:S(2)}, u32[]{:S(2)}) collective-permute-start(bf16[512,128]{1,0:T(8,128)(2,1)S(1)} %get-tuple-element.33), channel_id=1, source_target_pairs={{0,16},{16,0},{1,17},{17,1},{2,18},{18,2},{3,19},{19,3},{4,20},{20... | collective-permute-start | bytes 393224 | tf_op jit(solution)/shard_map/ppermute | solution.py:267
  98.1 32.9 %copy-start = (bf16[2048,1024]{1,0:T(8,128)(2,1)S(1)}, bf16[2048,1024]{1,0:T(8,128)(2,1)}, u32[]{:S(2)}) copy-start(bf16[2048,1024]{1,0:T(8,128)(2,1)} %refs_2_.5) | copy-start | bytes 12582916
  98.8 6.1 %collective-permute-start.23 = (bf16[256,256]{1,0:T(8,128)(2,1)S(1)}, bf16[256,256]{1,0:T(8,128)(2,1)S(1)}, u32[]{:S(2)}, u32[]{:S(2)}) collective-permute-start(bf16[256,256]{1,0:T(8,128)(2,1)S(1)} %get-tuple-element.44), channel_id=1, source_target_pairs={{0,4},{1,5},{2,6},{3,7},{4,0},{5,1},{6,2},{7,3},{8,12},{9,13},{10,... | collective-permute-start | bytes 393224 | tf_op jit(solution)/shard_map/ppermute | solution.py:264
  100.3 14.1 %collective-permute-start.24 = (bf16[256,256]{1,0:T(8,128)(2,1)S(1)}, bf16[256,256]{1,0:T(8,128)(2,1)S(1)}, u32[]{:S(2)}, u32[]{:S(2)}) collective-permute-start(bf16[256,256]{1,0:T(8,128)(2,1)S(1)} %get-tuple-element.45), channel_id=1, source_target_pairs={{0,8},{1,9},{2,10},{3,11},{4,12},{5,13},{6,14},{7,15},{8,0},{9,1},... | collective-permute-start | bytes 393224 | tf_op jit(solution)/shard_map/ppermute | solution.py:264
  103.7 15.1 %collective-permute-start.25 = (bf16[256,256]{1,0:T(8,128)(2,1)S(1)}, bf16[256,256]{1,0:T(8,128)(2,1)S(1)}, u32[]{:S(2)}, u32[]{:S(2)}) collective-permute-start(bf16[256,256]{1,0:T(8,128)(2,1)S(1)} %get-tuple-element.46), channel_id=1, source_target_pairs={{0,12},{1,13},{2,14},{3,15},{4,8},{5,9},{6,10},{7,11},{8,4},{9,5},... | collective-permute-start | bytes 393224 | tf_op jit(solution)/shard_map/ppermute | solution.py:264
  118.8 7.0 %collective-permute-start.26 = (bf16[512,256]{1,0:T(8,128)(2,1)S(1)}, bf16[512,256]{1,0:T(8,128)(2,1)S(1)}, u32[]{:S(2)}, u32[]{:S(2)}) collective-permute-start(bf16[512,256]{1,0:T(8,128)(2,1)S(1)} %shard_map.78), channel_id=1, source_target_pairs={{0,2},{1,3},{2,0},{3,1},{4,6},{5,7},{6,4},{7,5},{8,10},{9,11},{10,... | collective-permute-start | bytes 786440 | tf_op jit(solution)/shard_map/ppermute | solution.py:264
  120.0 15.3 %collective-permute-start.22 = (bf16[512,384]{1,0:T(8,128)(2,1)S(1)}, bf16[512,384]{1,0:T(8,128)(2,1)S(1)}, u32[]{:S(2)}, u32[]{:S(2)}) collective-permute-start(bf16[512,384]{1,0:T(8,128)(2,1)S(1)} %get-tuple-element.42.refs_1_), channel_id=1, source_target_pairs={{0,16},{16,0},{1,17},{17,1},{2,18},{18,2},{3,19},{19,3},{4,20},{20... | collective-permute-start | bytes 1179656 | tf_op jit(solution)/shard_map/ppermute | solution.py:267
  125.7 3.1 %collective-permute-start.27 = (bf16[512,256]{1,0:T(8,128)(2,1)S(1)}, bf16[512,256]{1,0:T(8,128)(2,1)S(1)}, u32[]{:S(2)}, u32[]{:S(2)}) collective-permute-start(bf16[512,256]{1,0:T(8,128)(2,1)S(1)} %shard_map.79), channel_id=1, source_target_pairs={{0,1},{1,0},{2,3},{3,2},{4,5},{5,4},{6,7},{7,6},{8,9},{9,8},{10,11... | collective-permute-start | bytes 786440 | tf_op jit(solution)/shard_map/ppermute | solution.py:264
  127.6 7.7 %collective-permute-start.19 = (bf16[512,128]{1,0:T(8,128)(2,1)S(1)}, bf16[512,128]{1,0:T(8,128)(2,1)S(1)}, u32[]{:S(2)}, u32[]{:S(2)}) collective-permute-start(bf16[512,128]{1,0:T(8,128)(2,1)S(1)} %get-tuple-element.37.refs_0_), channel_id=1, source_target_pairs={{0,16},{16,0},{1,17},{17,1},{2,18},{18,2},{3,19},{19,3},{4,20},{20... | collective-permute-start | bytes 393224 | tf_op jit(solution)/shard_map/ppermute | solution.py:267
  129.8 11.1 %collective-permute-start.28 = (bf16[128,128]{1,0:T(8,128)(2,1)S(1)}, bf16[128,128]{1,0:T(8,128)(2,1)S(1)}, u32[]{:S(2)}, u32[]{:S(2)}) collective-permute-start(bf16[128,128]{1,0:T(8,128)(2,1)S(1)} %get-tuple-element.51), channel_id=1, source_target_pairs={{0,16},{16,0},{1,17},{17,1},{2,18},{18,2},{3,19},{19,3},{4,20},{20... | collective-permute-start | bytes 98312 | tf_op jit(solution)/shard_map/ppermute | solution.py:267
